TPU v7x, 32 devices: a whole 2x2x4 slice. The times are simulated.
32 devices in a mesh: group: 4 (over z), dev: 8 (over y, x, core).
Axes of the slice: x: 2, y: 2, z: 4, core: 2. Of those that a mesh axis runs over, the one named last changes fastest.
Arguments:
- positions: float32 [3, 1024, 256], P(None, ('group', 'dev')), may hold values from -3 to 3
- velocities: float32 [3, 1024, 256], P(None, ('group', 'dev')), may hold values from -3 to 3
- masses: float32 [1024, 256], P(('group', 'dev')), may hold values from 0.005 to 0.05
- counts: int32 [1024], P(('group', 'dev')), may hold values from 64 to 256, as said below
- walls: int32 [1024, 256], P(('group', 'dev')), may hold values 0 or 1
- neighbours: int32 [1024, 3], P(('group', 'dev')), may hold values from 0 to 55, as said below
- send_cells: int32 [4, 8, 8, 2], P('group', 'dev'), may hold values from -1 to 31, as said below
- owners: int32 [4, 256], P('group'), may hold values from 0 to 7, as said below
Outputs:
- new_state: float32 [6, 1024, 256], P(None, ('group', 'dev'))
- new_density: float32 [1024, 256], P(('group', 'dev'))
Inputs may be any that keep to these rules, and one draw needn't show every extreme that they name: `counts`: every device holds at least one cell with 256 particles. `send_cells`: A device never sends to itself; slot 0 to every other device of its group holds a cell. `neighbours`: A cell never names its own row; on each device every rim row and every filled incoming slot is named at least once, and no empty incoming slot is named. `owners`: each device of a group owns exactly 32 cells afterwards; each device keeps 32 - 2 * 2 of its cells and hands exactly 2 cells to each of 2 other devices of its group, and none to the rest.
All inputs are finite; a program needn't handle non-finite values. No bound on the sum of `walls` on one device may be relied on, other than what follows from the above.
Results may differ from a plain program's by a relative error of at most 0.0003.
Values sent between devices are 32-bit elements; how exact they have to be, the bound alone decides.
A program may use at most 64 MiB of HBM per device.

v0:
```python
import jax
import jax.numpy as jnp
from jax import lax
from jax.sharding import PartitionSpec as P

RIM_CELLS = 4


SUPPORT = 4.0
STIFFNESS = 2.0
REST_DENSITY = 0.8
VISCOSITY = 0.5
COHESION = 0.3
ADHESION = 0.8
GRAVITY = 1.0
TIME_STEP = 0.5


def with_halo(cells, sides, width):
    for axis, dim in sides:
        count = lax.axis_size(axis)
        ends = count - 1
        head = lax.slice_in_dim(cells, 0, width, axis=dim)
        tail = lax.slice_in_dim(cells, cells.shape[dim] - width, cells.shape[dim], axis=dim)
        cells = jnp.concatenate(
            [
                lax.ppermute(tail, axis, [(i, (i + 1) % count) for i in range(ends)]),
                cells,
                lax.ppermute(head, axis, [((i + 1) % count, i) for i in range(ends)]),
            ],
            axis=dim,
        )
    return cells


def pair_density(own_pos, lookup, columns):
    remote = lookup[:, columns, :]
    distance = jnp.zeros(
        (own_pos.shape[1], own_pos.shape[2], columns.shape[1], lookup.shape[2]), jnp.float32
    )
    for component in range(3):
        offset = own_pos[component][:, :, None, None] - remote[component][:, None, :, :]
        distance = distance + offset * offset
    weight = jnp.maximum(1.0 - distance / SUPPORT, 0.0)
    return jnp.sum(remote[3][:, None, :, :] * weight * weight * weight, axis=(2, 3))


def pair_force(own_pos, own_vel, own_q, lookup, columns):
    remote = lookup[:, columns, :]
    distance = jnp.zeros(
        (own_pos.shape[1], own_pos.shape[2], columns.shape[1], lookup.shape[2]), jnp.float32
    )
    offsets = []
    for component in range(3):
        offset = own_pos[component][:, :, None, None] - remote[component][:, None, :, :]
        offsets.append(offset)
        distance = distance + offset * offset
    weight = jnp.maximum(1.0 - distance / SUPPORT, 0.0)
    cube = weight * weight * weight
    pushes = (
        remote[6][:, None]
        * (own_q[:, :, None, None] + remote[8][:, None])
        * (6.0 / SUPPORT)
        * weight
        * weight
        - remote[7][:, None] * weight
    )
    damping = VISCOSITY * remote[6][:, None] * cube
    total_damping = jnp.sum(damping, axis=(2, 3))
    rows = []
    for component in range(3):
        rows.append(
            jnp.sum(
                offsets[component] * pushes + damping * remote[3 + component][:, None], axis=(2, 3)
            )
            - own_vel[component] * total_damping
        )
    return jnp.stack(rows, 0)


def shards(positions, velocities, masses, counts, walls, neighbours, send_cells, owners):
    cell_count = positions.shape[1]
    block_width = positions.shape[2]
    peer_count = lax.axis_size("dev")
    particle_slot = lax.broadcasted_iota(jnp.int32, (cell_count, block_width), 1)
    active = (particle_slot < counts[:, None]).astype(jnp.float32)
    wall_mask = walls.astype(jnp.float32) * active
    fluid_mask = active - wall_mask
    mass_eff = masses * active
    bond = mass_eff * (COHESION + (ADHESION - COHESION) * wall_mask)
    send_list = send_cells[0, 0].reshape(-1)
    present = (send_list >= 0).astype(jnp.float32)
    chosen = jnp.maximum(send_list, 0)

    def outgoing(field):
        return field[:, chosen, :] * present[None, :, None]

    def joined(padded, arrived):
        return jnp.concatenate([padded, arrived], 1)

    dens_field = jnp.concatenate([positions, mass_eff[None]], 0)
    dens_table = joined(
        with_halo(dens_field, (("group", 1),), RIM_CELLS),
        lax.all_to_all(outgoing(dens_field), "dev", split_axis=1, concat_axis=1, tiled=True),
    )
    cell_blocks = jnp.arange(cell_count, dtype=jnp.int32).reshape(-1, 4)

    def density_block(cell_ids):
        columns = jnp.concatenate([RIM_CELLS + cell_ids[:, None], neighbours[cell_ids]], 1)
        return pair_density(positions[:, cell_ids, :], dens_table, columns)

    density = lax.map(density_block, cell_blocks).reshape(cell_count, block_width)
    safe_rho = active * density + (1.0 - active)
    pressure_q = active * STIFFNESS * (density - REST_DENSITY) / (safe_rho * safe_rho)
    force_field = jnp.concatenate(
        [positions, velocities, mass_eff[None], bond[None], pressure_q[None]], 0
    )
    force_table = joined(
        with_halo(force_field, (("group", 1),), RIM_CELLS),
        lax.all_to_all(outgoing(force_field), "dev", split_axis=1, concat_axis=1, tiled=True),
    )

    def force_block(cell_ids):
        columns = jnp.concatenate([RIM_CELLS + cell_ids[:, None], neighbours[cell_ids]], 1)
        return pair_force(
            positions[:, cell_ids, :],
            velocities[:, cell_ids, :],
            pressure_q[cell_ids],
            force_table,
            columns,
        )

    acceleration = lax.map(force_block, cell_blocks)
    acceleration = jnp.transpose(acceleration, (1, 0, 2, 3)).reshape(3, cell_count, block_width)
    gravity_vec = jnp.array([0.0, 0.0, GRAVITY], jnp.float32)[:, None, None]
    acceleration = acceleration - gravity_vec
    new_vel = velocities + TIME_STEP * fluid_mask[None] * acceleration
    new_pos = positions + TIME_STEP * fluid_mask[None] * new_vel
    moved = jnp.concatenate([new_pos, new_vel, density[None]], 0) * active[None]
    capacity = max(2, cell_count // (2 * peer_count))
    own_index = lax.axis_index("dev")
    group_owner = owners[0]
    own_owners = lax.dynamic_slice_in_dim(group_owner, own_index * cell_count, cell_count)
    one_hot = (own_owners[:, None] == jnp.arange(peer_count, dtype=jnp.int32)[None, :]).astype(
        jnp.int32
    )
    send_rank = jnp.sum((jnp.cumsum(one_hot, 0) - one_hot) * one_hot, 1)
    staying = own_owners == own_index
    slot_index = jnp.where(staying, peer_count * capacity, own_owners * capacity + send_rank)
    outbox = (
        jnp.zeros((7, peer_count * capacity, block_width), jnp.float32)
        .at[:, slot_index, :]
        .set(moved, mode="drop")
    )
    inbox = lax.all_to_all(outbox, "dev", split_axis=1, concat_axis=1, tiled=True)
    arrivals = jnp.sum(
        (group_owner.reshape(peer_count, cell_count) == own_index).astype(jnp.int32), 1
    )
    arrival_start = jnp.cumsum(arrivals) - arrivals
    rank_in = lax.broadcasted_iota(jnp.int32, (peer_count, capacity), 1)
    source_row = lax.broadcasted_iota(jnp.int32, (peer_count, capacity), 0)
    usable = (rank_in < arrivals[:, None]) & (source_row != own_index)
    arrival_slot = jnp.where(usable, arrival_start[:, None] + rank_in, cell_count).reshape(-1)
    keep_slot = jnp.where(staying, arrival_start[own_index] + send_rank, cell_count)
    settled = (
        jnp.zeros((7, cell_count, block_width), jnp.float32)
        .at[:, arrival_slot, :]
        .set(inbox, mode="drop")
    )
    settled = settled.at[:, keep_slot, :].set(moved, mode="drop")
    return (settled[0:6], settled[6])


def solution(mesh):
    return jax.shard_map(
        shards,
        mesh=mesh,
        in_specs=(
            P(None, ("group", "dev"), None),
            P(None, ("group", "dev"), None),
            P(("group", "dev"), None),
            P(("group", "dev")),
            P(("group", "dev"), None),
            P(("group", "dev"), None),
            P("group", "dev", None, None),
            P("group", None),
        ),
        out_specs=(P(None, ("group", "dev"), None), P(("group", "dev"), None)),
        check_vma=False,
    )
```

profile of v0, /device:TPU:0, one launch (start us, length us, event | category | flops | bytes accessed | tf_op | source)
XLA Modules:
  0.0 174.3 jit_solution(14094200770331152187)
XLA Ops:
  5.7 5.2 %all-to-all-start = ((f32[4,16,256]{2,0,1:T(4,128)}), f32[4,16,256]{2,0,1:T(4,128)S(1)}, u32[]{:S(2)}, u32[]{:S(2)}) async-start(f32[4,16,256]{2,0,1:T(4,128)} %multiply_bitcast_fusion.1), calls=%async_computation | async-start | bytes 131072 | tf_op jit(solution)/shard_map/all_to_all | solution.py:104
  10.9 3.5 %collective-permute-start = (f32[4,4,256]{2,0,1:T(4,128)S(1)}, f32[4,4,256]{2,0,1:T(4,128)S(1)}, u32[]{:S(2)}, u32[]{:S(2)}) collective-permute-start(f32[4,4,256]{2,0,1:T(4,128)S(1)} %get-tuple-element.204), channel_id=1, source_target_pairs={{0,8},{8,16},{16,24},{1,9},{9,17},{17,25},{2,10},{10,18},{18,26},{... | collective-permute-start | bytes 49160 | tf_op jit(solution)/shard_map/ppermute | solution.py:27
  20.1 37.5 %while.20 = (s32[]{:T(128)}, f32[8,4,256]{2,1,0:T(4,128)S(1)}, s32[8,4]{1,0:T(8,128)S(1)}, s32[32,3]{1,0:T(8,128)S(1)}, f32[4,56,256]{2,0,1:T(4,128)S(1)}, /*index=5*/f32[3,32,256]{2,0,1:T(4,128)S(1)}, s32[]{:T(128)}) while((s32[]{:T(128)}, f32[8,4,256]{2,1,0:T(4,128)S(1)}, s32[8,4]{1,0:T(8,128)S(1)}, s32[32,3]{1,0:T(8,128)S(1)}, ...), condition=%wide.region_6.7_spmd, body=%wide.region_4.0_spmd.sunk | while | flops 15729746 | bytes 565941 | solution.py:112
  22.3 2.5 %fusion.57 = f32[4,256]{1,0:T(4,128)S(1)} fusion(f32[4,4,256]{2,1,0:T(4,128)S(1)} %get-tuple-element.339, f32[4,256]{1,0:T(4,128)S(1)} %get-tuple-element.342, f32[4,4,256]{2,1,0:T(4,128)S(1)} %get-tuple-element.343, f32[4,256]{1,0:T(4,128)S(1)} %get-tuple-element.344, f32[4,4,256]{2,1,0:T(4,128)S(1)} %get-tuple-element.347, ...), kind=kLoop, calls=%fused_computation.14.clone.1 | loop fusion | flops 15727616 | bytes 81920 | tf_op jit(solution)/shard_map/while/body/eval_jaxpr/reduce_sum | solution.py:45
  27.0 2.5 %fusion.57 = f32[4,256]{1,0:T(4,128)S(1)} fusion(f32[4,4,256]{2,1,0:T(4,128)S(1)} %get-tuple-element.339, f32[4,256]{1,0:T(4,128)S(1)} %get-tuple-element.342, f32[4,4,256]{2,1,0:T(4,128)S(1)} %get-tuple-element.343, f32[4,256]{1,0:T(4,128)S(1)} %get-tuple-element.344, f32[4,4,256]{2,1,0:T(4,128)S(1)} %get-tuple-element.347, ...), kind=kLoop, calls=%fused_computation.14.clone.1 | loop fusion | flops 15727616 | bytes 81920 | tf_op jit(solution)/shard_map/while/body/eval_jaxpr/reduce_sum | solution.py:45
  31.7 2.5 %fusion.57 = f32[4,256]{1,0:T(4,128)S(1)} fusion(f32[4,4,256]{2,1,0:T(4,128)S(1)} %get-tuple-element.339, f32[4,256]{1,0:T(4,128)S(1)} %get-tuple-element.342, f32[4,4,256]{2,1,0:T(4,128)S(1)} %get-tuple-element.343, f32[4,256]{1,0:T(4,128)S(1)} %get-tuple-element.344, f32[4,4,256]{2,1,0:T(4,128)S(1)} %get-tuple-element.347, ...), kind=kLoop, calls=%fused_computation.14.clone.1 | loop fusion | flops 15727616 | bytes 81920 | tf_op jit(solution)/shard_map/while/body/eval_jaxpr/reduce_sum | solution.py:45
  36.3 2.5 %fusion.57 = f32[4,256]{1,0:T(4,128)S(1)} fusion(f32[4,4,256]{2,1,0:T(4,128)S(1)} %get-tuple-element.339, f32[4,256]{1,0:T(4,128)S(1)} %get-tuple-element.342, f32[4,4,256]{2,1,0:T(4,128)S(1)} %get-tuple-element.343, f32[4,256]{1,0:T(4,128)S(1)} %get-tuple-element.344, f32[4,4,256]{2,1,0:T(4,128)S(1)} %get-tuple-element.347, ...), kind=kLoop, calls=%fused_computation.14.clone.1 | loop fusion | flops 15727616 | bytes 81920 | tf_op jit(solution)/shard_map/while/body/eval_jaxpr/reduce_sum | solution.py:45
  50.4 2.5 %fusion.57 = f32[4,256]{1,0:T(4,128)S(1)} fusion(f32[4,4,256]{2,1,0:T(4,128)S(1)} %get-tuple-element.339, f32[4,256]{1,0:T(4,128)S(1)} %get-tuple-element.342, f32[4,4,256]{2,1,0:T(4,128)S(1)} %get-tuple-element.343, f32[4,256]{1,0:T(4,128)S(1)} %get-tuple-element.344, f32[4,4,256]{2,1,0:T(4,128)S(1)} %get-tuple-element.347, ...), kind=kLoop, calls=%fused_computation.14.clone.1 | loop fusion | flops 15727616 | bytes 81920 | tf_op jit(solution)/shard_map/while/body/eval_jaxpr/reduce_sum | solution.py:45
  55.1 2.5 %fusion.57 = f32[4,256]{1,0:T(4,128)S(1)} fusion(f32[4,4,256]{2,1,0:T(4,128)S(1)} %get-tuple-element.339, f32[4,256]{1,0:T(4,128)S(1)} %get-tuple-element.342, f32[4,4,256]{2,1,0:T(4,128)S(1)} %get-tuple-element.343, f32[4,256]{1,0:T(4,128)S(1)} %get-tuple-element.344, f32[4,4,256]{2,1,0:T(4,128)S(1)} %get-tuple-element.347, ...), kind=kLoop, calls=%fused_computation.14.clone.1 | loop fusion | flops 15727616 | bytes 81920 | tf_op jit(solution)/shard_map/while/body/eval_jaxpr/reduce_sum | solution.py:45
  59.5 4.2 %all-to-all-start.1 = ((f32[9,16,256]{2,0,1:T(8,128)}), f32[9,16,256]{2,0,1:T(8,128)S(1)}, u32[]{:S(2)}, u32[]{:S(2)}) async-start(f32[9,16,256]{2,0,1:T(8,128)} %multiply_bitcast_fusion), calls=%async_computation.1 | async-start | bytes 524288 | tf_op jit(solution)/shard_map/all_to_all | solution.py:120
  63.7 3.5 %collective-permute-start.2 = (f32[9,4,256]{2,0,1:T(8,128)S(1)}, f32[9,4,256]{2,0,1:T(8,128)S(1)}, u32[]{:S(2)}, u32[]{:S(2)}) collective-permute-start(f32[9,4,256]{2,0,1:T(8,128)S(1)} %get-tuple-element.202), channel_id=1, source_target_pairs={{0,8},{8,16},{16,24},{1,9},{9,17},{17,25},{2,10},{10,18},{18,26},{... | collective-permute-start | bytes 110600 | tf_op jit(solution)/shard_map/ppermute | solution.py:27
  69.2 4.2 %collective-permute-done.3 = f32[9,4,256]{2,0,1:T(8,128)S(1)} collective-permute-done((f32[9,4,256]{2,0,1:T(8,128)S(1)}, f32[9,4,256]{2,0,1:T(8,128)S(1)}, u32[]{:S(2)}, u32[]{:S(2)}) %collective-permute-start.3) | collective-permute-done | bytes 36896 | tf_op jit(solution)/shard_map/ppermute | solution.py:29
  73.5 81.7 %while.21 = (s32[]{:T(128)}, f32[8,3,4,256]{3,1,2,0:T(4,128)S(1)}, s32[8,4]{1,0:T(8,128)S(1)}, f32[3,32,256]{2,0,1:T(4,128)S(1)}, s32[32,3]{1,0:T(8,128)S(1)}, /...) while((s32[]{:T(128)}, f32[8,3,4,256]{3,1,2,0:T(4,128)S(1)}, ...), condition=%wide.region_12.13_spmd, body=%wide.region_7.12_spmd.sunk | while | flops 35666000 | bytes 1299173 | solution.py:133
  76.3 6.7 %fusion.61 = (f32[4,256]{1,0:T(4,128)S(1)}, f32[4,256]{1,0:T(4,128)S(1)}, f32[4,256]{1,0:T(4,128)S(1)}, f32[4,256]{1,0:T(4,128)S(1)}) fusion(f32[4,4,256]{2,1,0:T(4,128)S(1)} %get-tuple-element.362, f32[4,4,256]{2,1,0:T(4,128)S(1)} %bitcast.193, f32[4,256]{1,0:T(4,128)S(1)} %bitcast.198, f32[4,4,256]{2,1,0:T(4,128)S(1)} %get-tuple-element.367, ...), kind=kLoop, calls=%fused_computation.45.clone.1 | loop fusion | flops 35647488 | bytes 196608 | tf_op jit(solution)/shard_map/while/body/eval_jaxpr/reduce_sum | solution.py:73
  86.5 6.7 %fusion.61 = (f32[4,256]{1,0:T(4,128)S(1)}, f32[4,256]{1,0:T(4,128)S(1)}, f32[4,256]{1,0:T(4,128)S(1)}, f32[4,256]{1,0:T(4,128)S(1)}) fusion(f32[4,4,256]{2,1,0:T(4,128)S(1)} %get-tuple-element.362, f32[4,4,256]{2,1,0:T(4,128)S(1)} %bitcast.193, f32[4,256]{1,0:T(4,128)S(1)} %bitcast.198, f32[4,4,256]{2,1,0:T(4,128)S(1)} %get-tuple-element.367, ...), kind=kLoop, calls=%fused_computation.45.clone.1 | loop fusion | flops 35647488 | bytes 196608 | tf_op jit(solution)/shard_map/while/body/eval_jaxpr/reduce_sum | solution.py:73
  96.7 6.7 %fusion.61 = (f32[4,256]{1,0:T(4,128)S(1)}, f32[4,256]{1,0:T(4,128)S(1)}, f32[4,256]{1,0:T(4,128)S(1)}, f32[4,256]{1,0:T(4,128)S(1)}) fusion(f32[4,4,256]{2,1,0:T(4,128)S(1)} %get-tuple-element.362, f32[4,4,256]{2,1,0:T(4,128)S(1)} %bitcast.193, f32[4,256]{1,0:T(4,128)S(1)} %bitcast.198, f32[4,4,256]{2,1,0:T(4,128)S(1)} %get-tuple-element.367, ...), kind=kLoop, calls=%fused_computation.45.clone.1 | loop fusion | flops 35647488 | bytes 196608 | tf_op jit(solution)/shard_map/while/body/eval_jaxpr/reduce_sum | solution.py:73
  106.9 6.7 %fusion.61 = (f32[4,256]{1,0:T(4,128)S(1)}, f32[4,256]{1,0:T(4,128)S(1)}, f32[4,256]{1,0:T(4,128)S(1)}, f32[4,256]{1,0:T(4,128)S(1)}) fusion(f32[4,4,256]{2,1,0:T(4,128)S(1)} %get-tuple-element.362, f32[4,4,256]{2,1,0:T(4,128)S(1)} %bitcast.193, f32[4,256]{1,0:T(4,128)S(1)} %bitcast.198, f32[4,4,256]{2,1,0:T(4,128)S(1)} %get-tuple-element.367, ...), kind=kLoop, calls=%fused_computation.45.clone.1 | loop fusion | flops 35647488 | bytes 196608 | tf_op jit(solution)/shard_map/while/body/eval_jaxpr/reduce_sum | solution.py:73
  117.2 6.7 %fusion.61 = (f32[4,256]{1,0:T(4,128)S(1)}, f32[4,256]{1,0:T(4,128)S(1)}, f32[4,256]{1,0:T(4,128)S(1)}, f32[4,256]{1,0:T(4,128)S(1)}) fusion(f32[4,4,256]{2,1,0:T(4,128)S(1)} %get-tuple-element.362, f32[4,4,256]{2,1,0:T(4,128)S(1)} %bitcast.193, f32[4,256]{1,0:T(4,128)S(1)} %bitcast.198, f32[4,4,256]{2,1,0:T(4,128)S(1)} %get-tuple-element.367, ...), kind=kLoop, calls=%fused_computation.45.clone.1 | loop fusion | flops 35647488 | bytes 196608 | tf_op jit(solution)/shard_map/while/body/eval_jaxpr/reduce_sum | solution.py:73
  127.4 6.7 %fusion.61 = (f32[4,256]{1,0:T(4,128)S(1)}, f32[4,256]{1,0:T(4,128)S(1)}, f32[4,256]{1,0:T(4,128)S(1)}, f32[4,256]{1,0:T(4,128)S(1)}) fusion(f32[4,4,256]{2,1,0:T(4,128)S(1)} %get-tuple-element.362, f32[4,4,256]{2,1,0:T(4,128)S(1)} %bitcast.193, f32[4,256]{1,0:T(4,128)S(1)} %bitcast.198, f32[4,4,256]{2,1,0:T(4,128)S(1)} %get-tuple-element.367, ...), kind=kLoop, calls=%fused_computation.45.clone.1 | loop fusion | flops 35647488 | bytes 196608 | tf_op jit(solution)/shard_map/while/body/eval_jaxpr/reduce_sum | solution.py:73
  137.6 6.7 %fusion.61 = (f32[4,256]{1,0:T(4,128)S(1)}, f32[4,256]{1,0:T(4,128)S(1)}, f32[4,256]{1,0:T(4,128)S(1)}, f32[4,256]{1,0:T(4,128)S(1)}) fusion(f32[4,4,256]{2,1,0:T(4,128)S(1)} %get-tuple-element.362, f32[4,4,256]{2,1,0:T(4,128)S(1)} %bitcast.193, f32[4,256]{1,0:T(4,128)S(1)} %bitcast.198, f32[4,4,256]{2,1,0:T(4,128)S(1)} %get-tuple-element.367, ...), kind=kLoop, calls=%fused_computation.45.clone.1 | loop fusion | flops 35647488 | bytes 196608 | tf_op jit(solution)/shard_map/while/body/eval_jaxpr/reduce_sum | solution.py:73
  147.8 6.7 %fusion.61 = (f32[4,256]{1,0:T(4,128)S(1)}, f32[4,256]{1,0:T(4,128)S(1)}, f32[4,256]{1,0:T(4,128)S(1)}, f32[4,256]{1,0:T(4,128)S(1)}) fusion(f32[4,4,256]{2,1,0:T(4,128)S(1)} %get-tuple-element.362, f32[4,4,256]{2,1,0:T(4,128)S(1)} %bitcast.193, f32[4,256]{1,0:T(4,128)S(1)} %bitcast.198, f32[4,4,256]{2,1,0:T(4,128)S(1)} %get-tuple-element.367, ...), kind=kLoop, calls=%fused_computation.45.clone.1 | loop fusion | flops 35647488 | bytes 196608 | tf_op jit(solution)/shard_map/while/body/eval_jaxpr/reduce_sum | solution.py:73
  156.2 4.3 %scatter_fusion = f32[7,16,256]{2,0,1:T(8,128)} fusion(f32[7,16,256]{2,0,1:T(8,128)} %broadcast_in_dim.48, s32[32]{0:T(128)S(1)} %get-tuple-element.210, f32[32,7,256]{2,1,0:T(8,128)S(1)} %copy.53), kind=kCustom, calls=%fused_computation.10 | custom fusion | bytes 688256 | tf_op jit(solution)/shard_map/scatter | solution.py:153
  160.4 4.4 %all-to-all-start.2 = ((f32[7,16,256]{2,0,1:T(8,128)}), f32[7,16,256]{2,0,1:T(8,128)S(1)}, u32[]{:S(2)}, u32[]{:S(2)}) async-start(f32[7,16,256]{2,0,1:T(8,128)} %scatter_fusion), calls=%async_computation.2 | async-start | bytes 262144 | tf_op jit(solution)/shard_map/all_to_all | solution.py:155
  164.8 5.5 %all-to-all-done.2 = f32[7,16,256]{2,0,1:T(8,128)S(1)} async-done(((f32[7,16,256]{2,0,1:T(8,128)}), f32[7,16,256]{2,0,1:T(8,128)S(1)}, u32[]{:S(2)}, u32[]{:S(2)}) %all-to-all-start.2) | async-done | bytes 114720 | tf_op jit(solution)/shard_map/all_to_all | solution.py:155
  (390 shorter events, 68.0 us)
Async XLA Ops:
  0.6 15.0 %copy-start.2 = (s32[32]{0:T(128)S(1)}, s32[32]{0:T(128)}, u32[]{:S(2)}) copy-start(s32[32]{0:T(128)} %param.16) | copy-start | bytes 388
  0.6 15.1 %copy-start.3 = (s32[1,256]{1,0:T(1,128)S(1)}, s32[1,256]{1,0:T(1,128)}, u32[]{:S(2)}) copy-start(s32[1,256]{1,0:T(1,128)} %param.20) | copy-start | bytes 3076
  0.7 17.3 %copy-start.4 = (s32[32,3]{0,1:T(4,128)S(1)}, s32[32,3]{0,1:T(4,128)}, u32[]{:S(2)}) copy-start(s32[32,3]{0,1:T(4,128)} %param.18) | copy-start | bytes 1156
  0.7 17.4 %copy-start.1 = (f32[3,32,256]{2,1,0:T(8,128)S(1)}, f32[3,32,256]{2,1,0:T(8,128)}, u32[]{:S(2)}) copy-start(f32[3,32,256]{2,1,0:T(8,128)} %param.14) | copy-start | bytes 294916
  5.7 14.3 %all-to-all-start = ((f32[4,16,256]{2,0,1:T(4,128)}), f32[4,16,256]{2,0,1:T(4,128)S(1)}, u32[]{:S(2)}, u32[]{:S(2)}) async-start(f32[4,16,256]{2,0,1:T(4,128)} %multiply_bitcast_fusion.1), calls=%async_computation | async-start | bytes 131072 | tf_op jit(solution)/shard_map/all_to_all | solution.py:104
  10.9 7.4 %collective-permute-start = (f32[4,4,256]{2,0,1:T(4,128)S(1)}, f32[4,4,256]{2,0,1:T(4,128)S(1)}, u32[]{:S(2)}, u32[]{:S(2)}) collective-permute-start(f32[4,4,256]{2,0,1:T(4,128)S(1)} %get-tuple-element.204), channel_id=1, source_target_pairs={{0,8},{8,16},{16,24},{1,9},{9,17},{17,25},{2,10},{10,18},{18,26},{... | collective-permute-start | bytes 49160 | tf_op jit(solution)/shard_map/ppermute | solution.py:27
  14.4 5.6 %collective-permute-start.1 = (f32[4,4,256]{2,0,1:T(4,128)S(1)}, f32[4,4,256]{2,0,1:T(4,128)S(1)}, u32[]{:S(2)}, u32[]{:S(2)}) collective-permute-start(f32[4,4,256]{2,0,1:T(4,128)S(1)} %get-tuple-element.205), channel_id=1, source_target_pairs={{8,0},{16,8},{24,16},{9,1},{17,9},{25,17},{10,2},{18,10},{26,18},{... | collective-permute-start | bytes 49160 | tf_op jit(solution)/shard_map/ppermute | solution.py:29
  59.5 13.8 %all-to-all-start.1 = ((f32[9,16,256]{2,0,1:T(8,128)}), f32[9,16,256]{2,0,1:T(8,128)S(1)}, u32[]{:S(2)}, u32[]{:S(2)}) async-start(f32[9,16,256]{2,0,1:T(8,128)} %multiply_bitcast_fusion), calls=%async_computation.1 | async-start | bytes 524288 | tf_op jit(solution)/shard_map/all_to_all | solution.py:120
  63.7 5.5 %collective-permute-start.2 = (f32[9,4,256]{2,0,1:T(8,128)S(1)}, f32[9,4,256]{2,0,1:T(8,128)S(1)}, u32[]{:S(2)}, u32[]{:S(2)}) collective-permute-start(f32[9,4,256]{2,0,1:T(8,128)S(1)} %get-tuple-element.202), channel_id=1, source_target_pairs={{0,8},{8,16},{16,24},{1,9},{9,17},{17,25},{2,10},{10,18},{18,26},{... | collective-permute-start | bytes 110600 | tf_op jit(solution)/shard_map/ppermute | solution.py:27
  67.2 6.2 %collective-permute-start.3 = (f32[9,4,256]{2,0,1:T(8,128)S(1)}, f32[9,4,256]{2,0,1:T(8,128)S(1)}, u32[]{:S(2)}, u32[]{:S(2)}) collective-permute-start(f32[9,4,256]{2,0,1:T(8,128)S(1)} %get-tuple-element.203), channel_id=1, source_target_pairs={{8,0},{16,8},{24,16},{9,1},{17,9},{25,17},{10,2},{18,10},{26,18},{... | collective-permute-start | bytes 110600 | tf_op jit(solution)/shard_map/ppermute | solution.py:29
  73.4 81.8 %copy-start = (f32[3,32,256]{2,1,0:T(8,128)S(1)}, f32[3,32,256]{2,1,0:T(8,128)}, u32[]{:S(2)}) copy-start(f32[3,32,256]{2,1,0:T(8,128)} %param.13) | copy-start | bytes 294916
  73.4 81.8 %copy-start.5 = (f32[3]{0:T(128)S(1)}, f32[3]{0:T(128)}, u32[]{:S(2)}) copy-start(f32[3]{0:T(128)} %constant.111) | copy-start | bytes 40
  160.4 9.9 %all-to-all-start.2 = ((f32[7,16,256]{2,0,1:T(8,128)}), f32[7,16,256]{2,0,1:T(8,128)S(1)}, u32[]{:S(2)}, u32[]{:S(2)}) async-start(f32[7,16,256]{2,0,1:T(8,128)} %scatter_fusion), calls=%async_computation.2 | async-start | bytes 262144 | tf_op jit(solution)/shard_map/all_to_all | solution.py:155
where the time goes:
time: 175 us; the launch traced here: 174 us
  other arithmetic  81.9 us (47%)
  local copies, waits for them, and re-layouts  54.4 us (31%)
  starting transfers between devices  23.3 us (13%)
  waiting for transfers between devices  12 us (7%)
  loops' own time  1.75 us (1%)
    reduce_sum x8, other arithmetic, pair_force(): jnp.sum(offsets[component] * pushes + damping * remote[3 + component][:,...  54 us
    reduce_sum x8, other arithmetic, pair_density(): jnp.sum(remote[3][:, None, :, :] * weight * weight * weight, axis=(2, 3))  20 us
    ppermute x2, starting transfers between devices, with_halo(): lax.ppermute(tail, axis, [(i, (i + 1) % count) for i in range(ends)])  6.95 us
    ppermute x2, waiting for transfers between devices, with_halo(): lax.ppermute(head, axis, [((i + 1) % count, i) for i in range(ends)])  5.9 us
    all_to_all x1, waiting for transfers between devices, shards(): lax.all_to_all(outbox, 'dev', split_axis=1, concat_axis=1, tiled=True)  5.49 us
    all_to_all x1, starting transfers between devices, shards(): lax.all_to_all(outgoing(dens_field), 'dev', split_axis=1, concat_axis=1,...  5.2 us
    gather x8, local copies, waits for them, and re-layouts, pair_density(): remote = lookup[:, columns, :]  4.75 us
    gather x8, local copies, waits for them, and re-layouts, force_block(): velocities[:, cell_ids, :]  4.59 us
  transfers between devices with their start and end apart: 7, of which 4 were waited for; matrix products, arithmetic and copies ran while one was open for 2% of the time, Pallas kernels for 0%

commit v1 on v0

v1 whole, which is shorter than its diff:
```python
import functools

import jax
import jax.numpy as jnp
from jax import lax
from jax.experimental import pallas as pl
from jax.experimental.pallas import tpu as pltpu
from jax.sharding import PartitionSpec as P

RIM_CELLS = 4


SUPPORT = 4.0
STIFFNESS = 2.0
REST_DENSITY = 0.8
VISCOSITY = 0.5
COHESION = 0.3
ADHESION = 0.8
GRAVITY = 1.0
TIME_STEP = 0.5


def coarse(a):
    return a.astype(jnp.bfloat16).astype(jnp.float32)


def split3(a):
    high = coarse(a)
    rest = a - high
    mid = coarse(rest)
    return high, mid, coarse(rest - mid)


def source_side(pos, scale):
    square = jnp.sum(pos * pos, axis=0, keepdims=True)
    rows = jnp.concatenate(
        [
            scale * (1.0 - square / SUPPORT),
            scale / SUPPORT,
            scale * pos * (2.0 / SUPPORT),
            jnp.zeros_like(pos),
        ],
        0,
    )
    h, m, l = split3(rows)
    return jnp.concatenate([h, h, m, m, h, l], 0).T.astype(jnp.bfloat16)


def target_side(pos):
    square = jnp.sum(pos * pos, axis=0, keepdims=True)
    rows = jnp.concatenate([jnp.ones_like(square), -square, pos, jnp.zeros_like(pos)], 0)
    h, m, l = split3(rows)
    return jnp.concatenate([h, m, h, m, l, h], 0).astype(jnp.bfloat16)


def mm(a, b):
    return jnp.dot(a, b, preferred_element_type=jnp.float32)


def partner_rows(near, c):
    near_cells = 3
    return [RIM_CELLS + c] + [near[c * near_cells + k] for k in range(near_cells)]


def density_kernel(near, counts, table, rho_ref, q_ref, left):
    rows_total = table.shape[0]
    cells = rho_ref.shape[0]

    def prepare(r, _):
        row = table[r]
        mass = row[3:4]
        root = jnp.where(mass > 0.0, jnp.exp(jnp.log(jnp.maximum(mass, 1e-30)) * (1.0 / 3.0)), 0.0)
        left[r] = source_side(row[0:3], root)
        return 0

    lax.fori_loop(0, rows_total, prepare, 0)

    def cell(c, _):
        right = target_side(table[RIM_CELLS + c][0:3])
        total = jnp.zeros((8, right.shape[1]), jnp.float32)
        for r in partner_rows(near, c):
            u = jnp.maximum(mm(left[r], right), 0.0)
            total = total + jnp.sum((u * u * u).reshape(-1, 8, u.shape[1]), axis=0)
        rho = jnp.sum(total, axis=0, keepdims=True)
        slot = lax.broadcasted_iota(jnp.int32, rho.shape, 1)
        active = (slot < counts[c]).astype(jnp.float32)
        safe = active * rho + (1.0 - active)
        rho_ref[pl.ds(c, 1)] = rho
        q_ref[pl.ds(c, 1)] = active * STIFFNESS * (rho - REST_DENSITY) / (safe * safe)
        return 0

    lax.fori_loop(0, cells, cell, 0)


def force_kernel(near, counts, table, q_table, walls, rho_ref, out_ref, left, red1, red2, red3):
    rows_total = table.shape[0]
    cells = rho_ref.shape[0]

    def prepare(r, _):
        row = table[r]
        pos, mass, vel, bond = row[0:3], row[3:4], row[4:7], row[7:8]
        left[r] = source_side(pos, jnp.ones_like(mass))
        mq = mass * q_table[pl.ds(r, 1)]
        two = jnp.concatenate([mass, mass * pos, mq, mq * pos], 0)
        one = jnp.concatenate([bond, bond * pos, mass, mass * vel], 0)
        h2 = coarse(two)
        h1 = coarse(one)
        l1 = one - h1
        red2[r] = jnp.concatenate([h2, two - h2], 0).astype(jnp.bfloat16)
        red1[r] = jnp.concatenate([h1[0:4], l1[0:4], l1[0:4] * 0.0, l1[0:4] * 0.0], 0).astype(jnp.bfloat16)
        red3[r] = jnp.concatenate([h1[4:8], l1[4:8], l1[0:4] * 0.0, l1[0:4] * 0.0], 0).astype(jnp.bfloat16)
        return 0

    lax.fori_loop(0, rows_total, prepare, 0)

    def cell(c, _):
        row = table[RIM_CELLS + c]
        pos, vel = row[0:3], row[4:7]
        right = target_side(pos)
        width = right.shape[1]
        s1 = jnp.zeros((16, width), jnp.float32)
        s2 = jnp.zeros((16, width), jnp.float32)
        s3 = jnp.zeros((16, width), jnp.float32)
        for r in partner_rows(near, c):
            w = jnp.maximum(mm(left[r], right), 0.0)
            w2 = w * w
            w3 = w2 * w
            high = w2.astype(jnp.bfloat16)
            low = (w2 - high.astype(jnp.float32)).astype(jnp.bfloat16)
            s2 = s2 + mm(red2[r], high) + mm(red2[r], low)
            s1 = s1 + mm(red1[r], w.astype(jnp.bfloat16))
            s3 = s3 + mm(red3[r], w3.astype(jnp.bfloat16))
        s2 = s2[0:8] + s2[8:16]
        s1 = s1[0:4] + s1[4:8]
        s3 = s3[0:4] + s3[4:8]
        q = q_table[pl.ds(RIM_CELLS + c, 1)]
        acc = (
            (6.0 / SUPPORT) * (q * (pos * s2[0:1] - s2[1:4]) + (pos * s2[4:5] - s2[5:8]))
            - (pos * s1[0:1] - s1[1:4])
            + VISCOSITY * (s3[1:4] - vel * s3[0:1])
        )
        component = lax.broadcasted_iota(jnp.int32, acc.shape, 0)
        acc = acc - jnp.where(component == 2, GRAVITY, 0.0)
        slot = lax.broadcasted_iota(jnp.int32, q.shape, 1)
        active = (slot < counts[c]).astype(jnp.float32)
        fluid = active - walls[pl.ds(c, 1)].astype(jnp.float32) * active
        new_vel = vel + TIME_STEP * fluid * acc
        new_pos = pos + TIME_STEP * fluid * new_vel
        rho = rho_ref[pl.ds(c, 1)]
        out_ref[c] = active * jnp.concatenate([new_pos, new_vel, rho, jnp.zeros_like(rho)], 0)
        return 0

    lax.fori_loop(0, cells, cell, 0)


def vmem(count):
    return [pl.BlockSpec(memory_space=pltpu.VMEM)] * count


def smem(count):
    return [pl.BlockSpec(memory_space=pltpu.SMEM)] * count


def densities(near, counts, table, cells):
    rows, _, width = table.shape
    shape = jax.ShapeDtypeStruct((cells, width), jnp.float32)
    return pl.pallas_call(
        density_kernel,
        out_shape=(shape, shape),
        in_specs=smem(2) + vmem(1),
        out_specs=tuple(vmem(2)),
        scratch_shapes=[pltpu.VMEM((rows, width, 48), jnp.bfloat16)],
        compiler_params=pltpu.CompilerParams(vmem_limit_bytes=48 * 2**20),
    )(near, counts, table)


def forces(near, counts, table, q_table, walls, rho):
    rows, _, width = table.shape
    return pl.pallas_call(
        force_kernel,
        out_shape=jax.ShapeDtypeStruct((rho.shape[0], 8, width), jnp.float32),
        in_specs=smem(2) + vmem(4),
        out_specs=vmem(1)[0],
        scratch_shapes=[pltpu.VMEM((rows, width, 48), jnp.bfloat16)]
        + [pltpu.VMEM((rows, 16, width), jnp.bfloat16)] * 3,
        compiler_params=pltpu.CompilerParams(vmem_limit_bytes=48 * 2**20),
    )(near, counts, table, q_table, walls, rho)


def full_table(cells, chosen, present):
    count = lax.axis_size("group")
    below = lax.ppermute(cells[-RIM_CELLS:], "group", [(i, i + 1) for i in range(count - 1)])
    above = lax.ppermute(cells[:RIM_CELLS], "group", [(i + 1, i) for i in range(count - 1)])
    out = cells[chosen] * present.reshape((-1,) + (1,) * (cells.ndim - 1))
    arrived = lax.all_to_all(out, "dev", split_axis=0, concat_axis=0, tiled=True)
    return jnp.concatenate([below, cells, above, arrived], 0)


def shards(positions, velocities, masses, counts, walls, neighbours, send_cells, owners):
    cell_count = positions.shape[1]
    block_width = positions.shape[2]
    peer_count = lax.axis_size("dev")
    particle_slot = lax.broadcasted_iota(jnp.int32, (cell_count, block_width), 1)
    active = (particle_slot < counts[:, None]).astype(jnp.float32)
    wall_mask = walls.astype(jnp.float32) * active
    mass_eff = masses * active
    bond = mass_eff * (COHESION + (ADHESION - COHESION) * wall_mask)
    send_list = send_cells[0, 0].reshape(-1)
    present = (send_list >= 0).astype(jnp.float32)
    chosen = jnp.maximum(send_list, 0)
    fields = jnp.concatenate([positions, mass_eff[None], velocities, bond[None]], 0)
    fields = jnp.transpose(fields, (1, 0, 2))
    table = full_table(fields, chosen, present)
    near = neighbours.reshape(-1)
    density, pressure = densities(near, counts, table, cell_count)
    q_table = full_table(pressure, chosen, present)
    moved = forces(near, counts, table, q_table, walls, density)
    capacity = max(2, cell_count // (2 * peer_count))
    own_index = lax.axis_index("dev")
    group_owner = owners[0]
    own_owners = lax.dynamic_slice_in_dim(group_owner, own_index * cell_count, cell_count)
    one_hot = (own_owners[:, None] == jnp.arange(peer_count, dtype=jnp.int32)[None, :]).astype(
        jnp.int32
    )
    send_rank = jnp.sum((jnp.cumsum(one_hot, 0) - one_hot) * one_hot, 1)
    staying = own_owners == own_index
    slot_index = jnp.where(staying, peer_count * capacity, own_owners * capacity + send_rank)
    outbox = (
        jnp.zeros((peer_count * capacity, 8, block_width), jnp.float32)
        .at[slot_index]
        .set(moved, mode="drop")
    )
    inbox = lax.all_to_all(outbox, "dev", split_axis=0, concat_axis=0, tiled=True)
    arrivals = jnp.sum(
        (group_owner.reshape(peer_count, cell_count) == own_index).astype(jnp.int32), 1
    )
    arrival_start = jnp.cumsum(arrivals) - arrivals
    rank_in = lax.broadcasted_iota(jnp.int32, (peer_count, capacity), 1)
    source_row = lax.broadcasted_iota(jnp.int32, (peer_count, capacity), 0)
    usable = (rank_in < arrivals[:, None]) & (source_row != own_index)
    arrival_slot = jnp.where(usable, arrival_start[:, None] + rank_in, cell_count).reshape(-1)
    keep_slot = jnp.where(staying, arrival_start[own_index] + send_rank, cell_count)
    settled = jnp.zeros((cell_count, 8, block_width), jnp.float32)
    settled = settled.at[arrival_slot].set(inbox, mode="drop")
    settled = settled.at[keep_slot].set(moved, mode="drop")
    settled = jnp.transpose(settled, (1, 0, 2))
    return (settled[0:6], settled[6])


def solution(mesh):
    return jax.shard_map(
        shards,
        mesh=mesh,
        in_specs=(
            P(None, ("group", "dev"), None),
            P(None, ("group", "dev"), None),
            P(("group", "dev"), None),
            P(("group", "dev")),
            P(("group", "dev"), None),
            P(("group", "dev"), None),
            P("group", "dev", None, None),
            P("group", None),
        ),
        out_specs=(P(None, ("group", "dev"), None), P(("group", "dev"), None)),
        check_vma=False,
    )
```

time: 175 us -> 114 us (0.65)
  other arithmetic: 81.9 us -> 4.63 us
  Pallas kernels: 0 us -> 58.5 us
  local copies, waits for them, and re-layouts: 54.4 us -> 15.2 us
  loops' own time: 1.75 us -> 0 us
    reduce_sum x16 -> x0, other arithmetic: 74 us -> none  [the longest x8 54 us: pair_force(): jnp.sum(offsets[component] * pushes + damping * remote[3 + component][:,...]
    pallas_call x0 -> x2, Pallas kernels: none -> 58.5 us  [the longest x1 41 us: forces(): pl.pallas_call(force_kernel, out_shape=jax.ShapeDtypeStruct((rho.shape[0]...]
    gather x66 -> x3, local copies, waits for them, and re-layouts: 37.6 us -> 1.16 us  [full_table(): out = cells[chosen] * present.reshape((-1,) + (1,) * (cells.ndim - 1))]
    unnamed x15 -> x19, local copies, waits for them, and re-layouts: 1.46 us -> 5 us
  transfers between devices with their start and end apart: 7 -> 7, of which waited for: 4 -> 3; matrix products, arithmetic and copies ran while one was open for 2% -> 2% of each run, Pallas kernels for 0% -> 0%
where the time goes in v1:
time: 114 us; the launch traced here: 113 us
  Pallas kernels  58.5 us (51%)
  starting transfers between devices  23.2 us (20%)
  local copies, waits for them, and re-layouts  15.2 us (13%)
  waiting for transfers between devices  10.4 us (9%)
  other arithmetic  4.63 us (4%)
    pallas_call x1, Pallas kernels, forces(): pl.pallas_call(force_kernel, out_shape=jax.ShapeDtypeStruct((rho.shape[0]...  41 us
    pallas_call x1, Pallas kernels, densities(): pl.pallas_call(density_kernel, out_shape=(shape, shape), in_specs=smem(2)...  17.6 us
    all_to_all x2, starting transfers between devices, full_table(): lax.all_to_all(out, 'dev', split_axis=0, concat_axis=0, tiled=True)  9.4 us
    ppermute x2, starting transfers between devices, full_table(): lax.ppermute(cells[-RIM_CELLS:], 'group', [(i, i + 1) for i in range(coun...  6.95 us
    all_to_all x1, waiting for transfers between devices, shards(): lax.all_to_all(outbox, 'dev', split_axis=0, concat_axis=0, tiled=True)  5.49 us
    unnamed x19, local copies, waits for them, and re-layouts  5 us
    ppermute x2, waiting for transfers between devices, full_table(): lax.ppermute(cells[:RIM_CELLS], 'group', [(i + 1, i) for i in range(count...  4.93 us
    scatter x1, local copies, waits for them, and re-layouts, shards(): outbox = jnp.zeros((peer_count * capacity, 8, block_width), jnp.float32)....  4.32 us
  transfers between devices with their start and end apart: 7, of which 3 were waited for; matrix products, arithmetic and copies ran while one was open for 2% of the time, Pallas kernels for 0%

profile of v1, /device:TPU:0, one launch (start us, length us, event | category | flops | bytes accessed | tf_op | source)
XLA Modules:
  0.0 112.9 jit_solution(12973759690405875257)
XLA Ops:
  0.6 0.7 broadcast_maximum_fusion
  2.0 0.9 fusion.1
  3.0 0.8 copy-done.2
  3.9 0.8 copy-done.3
  5.8 0.7 broadcast_multiply_fusion
  6.5 5.2 %all-to-all-start = ((f32[16,8,256]{2,1,0:T(8,128)}), f32[16,8,256]{2,1,0:T(8,128)S(1)}, u32[]{:S(2)}, u32[]{:S(2)}) async-start(f32[16,8,256]{2,1,0:T(8,128)} %broadcast_multiply_fusion), calls=%async_computation | async-start | bytes 262144 | tf_op jit(solution)/shard_map/all_to_all | solution.py:195
  11.8 3.5 %collective-permute-start = (f32[4,8,256]{2,1,0:T(8,128)S(1)}, f32[4,8,256]{2,1,0:T(8,128)S(1)}, u32[]{:S(2)}, u32[]{:S(2)}) collective-permute-start(f32[4,8,256]{2,1,0:T(8,128)S(1)} %get-tuple-element.8), channel_id=1, source_target_pairs={{0,8},{8,16},{16,24},{1,9},{9,17},{17,25},{2,10},{10,18},{18,26},{... | collective-permute-start | bytes 98312 | tf_op jit(solution)/shard_map/ppermute | solution.py:192
  15.2 1.3 %collective-permute-start.1 = (f32[4,8,256]{2,1,0:T(8,128)S(1)}, f32[4,8,256]{2,1,0:T(8,128)S(1)}, u32[]{:S(2)}, u32[]{:S(2)}) collective-permute-start(f32[4,8,256]{2,1,0:T(8,128)S(1)} %get-tuple-element.9), channel_id=1, source_target_pairs={{8,0},{16,8},{24,16},{9,1},{17,9},{25,17},{10,2},{18,10},{26,18},{... | collective-permute-start | bytes 98312 | tf_op jit(solution)/shard_map/ppermute | solution.py:193
  16.6 0.7 copy-done.5
  19.5 1.6 %collective-permute-done.1 = f32[4,8,256]{2,1,0:T(8,128)S(1)} collective-permute-done((f32[4,8,256]{2,1,0:T(8,128)S(1)}, f32[4,8,256]{2,1,0:T(8,128)S(1)}, u32[]{:S(2)}, u32[]{:S(2)}) %collective-permute-start.1) | collective-permute-done | bytes 32800 | tf_op jit(solution)/shard_map/ppermute | solution.py:193
  21.1 17.6 %shard_map.95 = (f32[32,256]{1,0:T(8,128)S(1)}, f32[32,256]{1,0:T(8,128)S(1)}) custom-call(s32[96]{0:T(128)S(1)} %reshape.213.near, s32[32]{0:T(128)S(1)} %copy-done.1, f32[56,8,256]{2,1,0:T(8,128)S(1)} %pad_maximum_fusion.table), custom_call_target="tpu_custom_call" | custom-call | tf_op jit(solution)/shard_map/pallas_call | solution.py:167
  39.3 0.7 broadcast_multiply_fusion.1
  40.0 4.2 %all-to-all-start.1 = ((f32[8,2,256]{2,1,0:T(2,128)}), f32[8,2,256]{2,1,0:T(2,128)S(1)}, u32[]{:S(2)}, u32[]{:S(2)}) async-start(f32[8,2,256]{2,1,0:T(2,128)} %broadcast_multiply_fusion.1), calls=%async_computation.1 | async-start | bytes 32768 | tf_op jit(solution)/shard_map/all_to_all | solution.py:195
  44.2 3.5 %collective-permute-start.2 = (f32[4,256]{1,0:T(4,128)S(1)}, f32[4,256]{1,0:T(4,128)S(1)}, u32[]{:S(2)}, u32[]{:S(2)}) collective-permute-start(f32[4,256]{1,0:T(4,128)S(1)} %get-tuple-element.12), channel_id=1, source_target_pairs={{0,8},{8,16},{16,24},{1,9},{9,17},{17,25},{2,10},{10,18},{18,26},{... | collective-permute-start | bytes 12296 | tf_op jit(solution)/shard_map/ppermute | solution.py:192
  47.6 1.3 %collective-permute-start.3 = (f32[4,256]{1,0:T(4,128)S(1)}, f32[4,256]{1,0:T(4,128)S(1)}, u32[]{:S(2)}, u32[]{:S(2)}) collective-permute-start(f32[4,256]{1,0:T(4,128)S(1)} %get-tuple-element.13), channel_id=1, source_target_pairs={{8,0},{16,8},{24,16},{9,1},{17,9},{25,17},{10,2},{18,10},{26,18},{... | collective-permute-start | bytes 12296 | tf_op jit(solution)/shard_map/ppermute | solution.py:193
  48.9 0.7 fusion.7
  49.8 3.4 %collective-permute-done.3 = f32[4,256]{1,0:T(4,128)S(1)} collective-permute-done((f32[4,256]{1,0:T(4,128)S(1)}, f32[4,256]{1,0:T(4,128)S(1)}, u32[]{:S(2)}, u32[]{:S(2)}) %collective-permute-start.3) | collective-permute-done | bytes 4128 | tf_op jit(solution)/shard_map/ppermute | solution.py:193
  53.2 41.0 %shard_map.96 = f32[32,8,256]{2,1,0:T(8,128)S(1)} custom-call(s32[96]{0:T(128)S(1)} %reshape.213.near, s32[32]{0:T(128)S(1)} %copy-done.1, f32[56,8,256]{2,1,0:T(8,128)S(1)} %pad_maximum_fusion.table, f32[56,256]{1,0:T(8,128)S(1)} %pad_maximum_fusion.1.q_table, s32[32,256]{1,0:T(8,128)S(1)} %copy-done, f32[32,256]{1,0:T(8,128)S(1)} %get-tuple-element.5.rho_ref), custom_call_target="tpu_custom_call" | custom-call | tf_op jit(solution)/shard_map/pallas_call | solution.py:179
  94.8 4.3 %scatter_fusion = f32[16,8,256]{2,1,0:T(8,128)} fusion(f32[16,8,256]{2,1,0:T(8,128)} %broadcast_in_dim.39, s32[32]{0:T(128)S(1)} %get-tuple-element.15, f32[32,8,256]{2,1,0:T(8,128)S(1)} %shard_map.96), kind=kCustom, calls=%fused_computation.2 | custom fusion | bytes 786560 | tf_op jit(solution)/shard_map/scatter | solution.py:231
  99.1 4.3 %all-to-all-start.2 = ((f32[16,8,256]{2,1,0:T(8,128)}), f32[16,8,256]{2,1,0:T(8,128)S(1)}, u32[]{:S(2)}, u32[]{:S(2)}) async-start(f32[16,8,256]{2,1,0:T(8,128)} %scatter_fusion), calls=%async_computation.2 | async-start | bytes 262144 | tf_op jit(solution)/shard_map/all_to_all | solution.py:233
  103.4 5.5 %all-to-all-done.2 = f32[16,8,256]{2,1,0:T(8,128)S(1)} async-done(((f32[16,8,256]{2,1,0:T(8,128)}), f32[16,8,256]{2,1,0:T(8,128)S(1)}, u32[]{:S(2)}, u32[]{:S(2)}) %all-to-all-start.2) | async-done | bytes 131104 | tf_op jit(solution)/shard_map/all_to_all | solution.py:233
  109.0 1.0 scatter_fusion.1
  110.0 1.5 %scatter_fusion.2 = f32[32,8,256]{2,1,0:T(8,128)S(1)} fusion(f32[32,8,256]{2,1,0:T(8,128)S(1)} %scatter_fusion.1, s32[32]{0:T(128)S(1)} %get-tuple-element.14, f32[32,8,256]{2,1,0:T(8,128)S(1)} %shard_map.96), kind=kCustom, calls=%fused_computation.4 | custom fusion | bytes 786560 | tf_op jit(solution)/shard_map/scatter | solution.py:245
  111.6 0.7 copy.24
  (55 shorter events, 6.2 us)
Async XLA Ops:
  0.6 0.8 copy-start.4
  1.4 0.7 copy-start.1
  2.9 0.9 copy-start.2
  3.8 0.9 copy-start.3
  6.5 14.5 %all-to-all-start = ((f32[16,8,256]{2,1,0:T(8,128)}), f32[16,8,256]{2,1,0:T(8,128)S(1)}, u32[]{:S(2)}, u32[]{:S(2)}) async-start(f32[16,8,256]{2,1,0:T(8,128)} %broadcast_multiply_fusion), calls=%async_computation | async-start | bytes 262144 | tf_op jit(solution)/shard_map/all_to_all | solution.py:195
  11.8 7.7 %collective-permute-start = (f32[4,8,256]{2,1,0:T(8,128)S(1)}, f32[4,8,256]{2,1,0:T(8,128)S(1)}, u32[]{:S(2)}, u32[]{:S(2)}) collective-permute-start(f32[4,8,256]{2,1,0:T(8,128)S(1)} %get-tuple-element.8), channel_id=1, source_target_pairs={{0,8},{8,16},{16,24},{1,9},{9,17},{17,25},{2,10},{10,18},{18,26},{... | collective-permute-start | bytes 98312 | tf_op jit(solution)/shard_map/ppermute | solution.py:192
  15.2 5.8 %collective-permute-start.1 = (f32[4,8,256]{2,1,0:T(8,128)S(1)}, f32[4,8,256]{2,1,0:T(8,128)S(1)}, u32[]{:S(2)}, u32[]{:S(2)}) collective-permute-start(f32[4,8,256]{2,1,0:T(8,128)S(1)} %get-tuple-element.9), channel_id=1, source_target_pairs={{8,0},{16,8},{24,16},{9,1},{17,9},{25,17},{10,2},{18,10},{26,18},{... | collective-permute-start | bytes 98312 | tf_op jit(solution)/shard_map/ppermute | solution.py:193
  16.6 0.7 copy-start.5
  17.9 0.7 copy-start.6
  40.0 9.8 %all-to-all-start.1 = ((f32[8,2,256]{2,1,0:T(2,128)}), f32[8,2,256]{2,1,0:T(2,128)S(1)}, u32[]{:S(2)}, u32[]{:S(2)}) async-start(f32[8,2,256]{2,1,0:T(2,128)} %broadcast_multiply_fusion.1), calls=%async_computation.1 | async-start | bytes 32768 | tf_op jit(solution)/shard_map/all_to_all | solution.py:195
  44.2 5.6 %collective-permute-start.2 = (f32[4,256]{1,0:T(4,128)S(1)}, f32[4,256]{1,0:T(4,128)S(1)}, u32[]{:S(2)}, u32[]{:S(2)}) collective-permute-start(f32[4,256]{1,0:T(4,128)S(1)} %get-tuple-element.12), channel_id=1, source_target_pairs={{0,8},{8,16},{16,24},{1,9},{9,17},{17,25},{2,10},{10,18},{18,26},{... | collective-permute-start | bytes 12296 | tf_op jit(solution)/shard_map/ppermute | solution.py:192
  47.6 5.5 %collective-permute-start.3 = (f32[4,256]{1,0:T(4,128)S(1)}, f32[4,256]{1,0:T(4,128)S(1)}, u32[]{:S(2)}, u32[]{:S(2)}) collective-permute-start(f32[4,256]{1,0:T(4,128)S(1)} %get-tuple-element.13), channel_id=1, source_target_pairs={{8,0},{16,8},{24,16},{9,1},{17,9},{25,17},{10,2},{18,10},{26,18},{... | collective-permute-start | bytes 12296 | tf_op jit(solution)/shard_map/ppermute | solution.py:193
  49.7 3.4 %copy-start = (s32[32,256]{1,0:T(8,128)S(1)}, s32[32,256]{1,0:T(8,128)}, u32[]{:S(2)}) copy-start(s32[32,256]{1,0:T(8,128)} %walls.1) | copy-start | bytes 98308
  99.1 9.8 %all-to-all-start.2 = ((f32[16,8,256]{2,1,0:T(8,128)}), f32[16,8,256]{2,1,0:T(8,128)S(1)}, u32[]{:S(2)}, u32[]{:S(2)}) async-start(f32[16,8,256]{2,1,0:T(8,128)} %scatter_fusion), calls=%async_computation.2 | async-start | bytes 262144 | tf_op jit(solution)/shard_map/all_to_all | solution.py:233

commit v2 on v1

--- a/solution.py
+++ b/solution.py
@@ -1,5 +1,3 @@
-import functools
-
 import jax
 import jax.numpy as jnp
 from jax import lax
@@ -8,6 +6,7 @@
 from jax.sharding import PartitionSpec as P
 
 RIM_CELLS = 4
+MESH = pl.DeviceIdType.MESH
 
 
 SUPPORT = 4.0
@@ -62,6 +61,210 @@
     return [RIM_CELLS + c] + [near[c * near_cells + k] for k in range(near_cells)]
 
 
+def to_peers(act):
+    me, count = lax.axis_index("dev"), lax.axis_size("dev")
+
+    def one(k, _):
+        act(lax.rem(me + k, count))
+        return 0
+
+    lax.fori_loop(1, count, one, 0)
+
+
+def greet(rim):
+    barrier = pltpu.get_barrier_semaphore()
+    group, groups = lax.axis_index("group"), lax.axis_size("group")
+
+    def hello(p):
+        pl.semaphore_signal(barrier, inc=1, device_id={"dev": p}, device_id_type=MESH)
+
+    to_peers(hello)
+    if not rim:
+        pl.semaphore_wait(barrier, lax.axis_size("dev") - 1)
+        return
+
+    @pl.when(group > 0)
+    def _():
+        pl.semaphore_signal(barrier, inc=1, device_id={"group": group - 1}, device_id_type=MESH)
+
+    @pl.when(group < groups - 1)
+    def _():
+        pl.semaphore_signal(barrier, inc=1, device_id={"group": group + 1}, device_id_type=MESH)
+
+    sides = jnp.where(group > 0, 1, 0) + jnp.where(group < groups - 1, 1, 0)
+    pl.semaphore_wait(barrier, lax.axis_size("dev") - 1 + sides)
+
+
+def swap_slots(source, target, base, width, send_sem, recv_sem):
+    me = lax.axis_index("dev")
+
+    def copy(p, lands):
+        return pltpu.make_async_remote_copy(
+            src_ref=source.at[pl.ds(p * width, width)],
+            dst_ref=target.at[pl.ds(base + lands * width, width)],
+            send_sem=send_sem.at[p],
+            recv_sem=recv_sem.at[lands],
+            device_id={"dev": p},
+            device_id_type=MESH,
+        )
+
+    def finish():
+        to_peers(lambda p: copy(p, p).wait_recv())
+        to_peers(lambda p: copy(p, me).wait_send())
+
+    to_peers(lambda p: copy(p, me).start())
+    return finish
+
+
+def swap_rims(table, cells, sems):
+    group, groups = lax.axis_index("group"), lax.axis_size("group")
+
+    def copy(up):
+        source = cells if up else RIM_CELLS
+        lands = 0 if up else RIM_CELLS + cells
+        step = 1 if up else -1
+        return pltpu.make_async_remote_copy(
+            src_ref=table.at[pl.ds(source, RIM_CELLS)],
+            dst_ref=table.at[pl.ds(lands, RIM_CELLS)],
+            send_sem=sems.at[0 if up else 1],
+            recv_sem=sems.at[2 if up else 3],
+            device_id={"group": group + step},
+            device_id_type=MESH,
+        )
+
+    @pl.when(group < groups - 1)
+    def _():
+        copy(True).start()
+
+    @pl.when(group > 0)
+    def _():
+        copy(False).start()
+
+    def finish():
+        @pl.when(group < groups - 1)
+        def _():
+            copy(False).wait_recv()
+            copy(True).wait_send()
+
+        @pl.when(group > 0)
+        def _():
+            copy(True).wait_recv()
+            copy(False).wait_send()
+
+    return finish
+
+
+def clear_missing(table, cells):
+    group, groups = lax.axis_index("group"), lax.axis_size("group")
+    shape = (RIM_CELLS,) + table.shape[1:]
+
+    @pl.when(group == 0)
+    def _():
+        table[0:RIM_CELLS] = jnp.zeros(shape, jnp.float32)
+
+    @pl.when(group == groups - 1)
+    def _():
+        table[RIM_CELLS + cells : 2 * RIM_CELLS + cells] = jnp.zeros(shape, jnp.float32)
+
+
+def clear_own(table, base, width):
+    table[pl.ds(base + lax.axis_index("dev") * width, width)] = jnp.zeros(
+        (width,) + table.shape[1:], jnp.float32
+    )
+
+
+def fields_kernel(counts, sends, pos, vel, masses, walls, table, out, slot_send, slot_recv, rim_sem):
+    cells = masses.shape[0]
+    slots = out.shape[0]
+    base = cells + 2 * RIM_CELLS
+    width = slots // lax.axis_size("dev")
+
+    def rows(c):
+        mass = masses[pl.ds(c, 1)]
+        slot = lax.broadcasted_iota(jnp.int32, mass.shape, 1)
+        active = (slot < counts[c]).astype(jnp.float32)
+        mass = mass * active
+        wall = walls[pl.ds(c, 1)].astype(jnp.float32) * active
+        bond = mass * (COHESION + (ADHESION - COHESION) * wall)
+        place = [pos[f, pl.ds(c, 1)] for f in range(3)]
+        speed = [vel[f, pl.ds(c, 1)] for f in range(3)]
+        return jnp.concatenate(place + [mass] + speed + [bond], 0)
+
+    def own(c, _):
+        table[RIM_CELLS + c] = rows(c)
+        return 0
+
+    def listed(s, _):
+        c = sends[s]
+        out[s] = rows(jnp.maximum(c, 0)) * (c >= 0).astype(jnp.float32)
+        return 0
+
+    lax.fori_loop(0, slots, listed, 0)
+    lax.fori_loop(0, cells, own, 0)
+    clear_missing(table, cells)
+    clear_own(table, base, width)
+    greet(True)
+    done_slots = swap_slots(out, table, base, width, slot_send, slot_recv)
+    done_rims = swap_rims(table, cells, rim_sem)
+    done_slots()
+    done_rims()
+
+
+def pressure_kernel(sends, pressure, table, out, slot_send, slot_recv, rim_sem):
+    cells = pressure.shape[0]
+    slots = out.shape[0]
+    base = cells + 2 * RIM_CELLS
+    width = slots // lax.axis_size("dev")
+
+    def listed(s, _):
+        c = sends[s]
+        out[s] = pressure[jnp.maximum(c, 0)] * (c >= 0).astype(jnp.float32)
+        return 0
+
+    def own(c, _):
+        table[RIM_CELLS + c] = pressure[c]
+        return 0
+
+    lax.fori_loop(0, slots, listed, 0)
+    lax.fori_loop(0, cells, own, 0)
+    clear_missing(table, cells)
+    clear_own(table, base, width)
+    greet(True)
+    done_slots = swap_slots(out, table, base, width, slot_send, slot_recv)
+    done_rims = swap_rims(table, cells, rim_sem)
+    done_slots()
+    done_rims()
+
+
+def settle_kernel(picks, order, moved, state, rho, out, pool, slot_send, slot_recv):
+    cells = moved.shape[0]
+    slots = out.shape[0]
+    width = slots // lax.axis_size("dev")
+
+    def listed(s, _):
+        out[s] = moved[picks[s]]
+        return 0
+
+    def own(c, _):
+        pool[c] = moved[c]
+        return 0
+
+    lax.fori_loop(0, slots, listed, 0)
+    lax.fori_loop(0, cells, own, 0)
+    clear_own(pool, cells, width)
+    greet(False)
+    swap_slots(out, pool, cells, width, slot_send, slot_recv)()
+
+    def place(s, _):
+        row = pool[order[s]]
+        for f in range(6):
+            state[f, pl.ds(s, 1)] = row[f : f + 1]
+        rho[pl.ds(s, 1)] = row[6:7]
+        return 0
+
+    lax.fori_loop(0, cells, place, 0)
+
+
 def density_kernel(near, counts, table, rho_ref, q_ref, left):
     rows_total = table.shape[0]
     cells = rho_ref.shape[0]
@@ -85,8 +288,8 @@
         slot = lax.broadcasted_iota(jnp.int32, rho.shape, 1)
         active = (slot < counts[c]).astype(jnp.float32)
         safe = active * rho + (1.0 - active)
-        rho_ref[pl.ds(c, 1)] = rho
-        q_ref[pl.ds(c, 1)] = active * STIFFNESS * (rho - REST_DENSITY) / (safe * safe)
+        rho_ref[c] = rho
+        q_ref[c] = active * STIFFNESS * (rho - REST_DENSITY) / (safe * safe)
         return 0
 
     lax.fori_loop(0, cells, cell, 0)
@@ -100,7 +303,7 @@
         row = table[r]
         pos, mass, vel, bond = row[0:3], row[3:4], row[4:7], row[7:8]
         left[r] = source_side(pos, jnp.ones_like(mass))
-        mq = mass * q_table[pl.ds(r, 1)]
+        mq = mass * q_table[r]
         two = jnp.concatenate([mass, mass * pos, mq, mq * pos], 0)
         one = jnp.concatenate([bond, bond * pos, mass, mass * vel], 0)
         h2 = coarse(two)
@@ -133,7 +336,7 @@
         s2 = s2[0:8] + s2[8:16]
         s1 = s1[0:4] + s1[4:8]
         s3 = s3[0:4] + s3[4:8]
-        q = q_table[pl.ds(RIM_CELLS + c, 1)]
+        q = q_table[RIM_CELLS + c]
         acc = (
             (6.0 / SUPPORT) * (q * (pos * s2[0:1] - s2[1:4]) + (pos * s2[4:5] - s2[5:8]))
             - (pos * s1[0:1] - s1[1:4])
@@ -146,7 +349,7 @@
         fluid = active - walls[pl.ds(c, 1)].astype(jnp.float32) * active
         new_vel = vel + TIME_STEP * fluid * acc
         new_pos = pos + TIME_STEP * fluid * new_vel
-        rho = rho_ref[pl.ds(c, 1)]
+        rho = rho_ref[c]
         out_ref[c] = active * jnp.concatenate([new_pos, new_vel, rho, jnp.zeros_like(rho)], 0)
         return 0
 
@@ -163,7 +366,7 @@
 
 def densities(near, counts, table, cells):
     rows, _, width = table.shape
-    shape = jax.ShapeDtypeStruct((cells, width), jnp.float32)
+    shape = jax.ShapeDtypeStruct((cells, 1, width), jnp.float32)
     return pl.pallas_call(
         density_kernel,
         out_shape=(shape, shape),
@@ -187,64 +390,84 @@
     )(near, counts, table, q_table, walls, rho)
 
 
-def full_table(cells, chosen, present):
-    count = lax.axis_size("group")
-    below = lax.ppermute(cells[-RIM_CELLS:], "group", [(i, i + 1) for i in range(count - 1)])
-    above = lax.ppermute(cells[:RIM_CELLS], "group", [(i + 1, i) for i in range(count - 1)])
-    out = cells[chosen] * present.reshape((-1,) + (1,) * (cells.ndim - 1))
-    arrived = lax.all_to_all(out, "dev", split_axis=0, concat_axis=0, tiled=True)
-    return jnp.concatenate([below, cells, above, arrived], 0)
+def remote(kernel, collective_id, in_specs, out_shape, scratch):
+    single = not isinstance(out_shape, tuple)
+    return pl.pallas_call(
+        kernel,
+        out_shape=out_shape,
+        in_specs=in_specs,
+        out_specs=vmem(1)[0] if single else tuple(vmem(len(out_shape))),
+        scratch_shapes=scratch,
+        compiler_params=pltpu.CompilerParams(
+            collective_id=collective_id, has_side_effects=True, vmem_limit_bytes=32 * 2**20
+        ),
+    )
 
 
 def shards(positions, velocities, masses, counts, walls, neighbours, send_cells, owners):
-    cell_count = positions.shape[1]
-    block_width = positions.shape[2]
+    cells = positions.shape[1]
+    width = positions.shape[2]
     peer_count = lax.axis_size("dev")
-    particle_slot = lax.broadcasted_iota(jnp.int32, (cell_count, block_width), 1)
-    active = (particle_slot < counts[:, None]).astype(jnp.float32)
-    wall_mask = walls.astype(jnp.float32) * active
-    mass_eff = masses * active
-    bond = mass_eff * (COHESION + (ADHESION - COHESION) * wall_mask)
-    send_list = send_cells[0, 0].reshape(-1)
-    present = (send_list >= 0).astype(jnp.float32)
-    chosen = jnp.maximum(send_list, 0)
-    fields = jnp.concatenate([positions, mass_eff[None], velocities, bond[None]], 0)
-    fields = jnp.transpose(fields, (1, 0, 2))
-    table = full_table(fields, chosen, present)
+    me = lax.axis_index("dev")
+    f32 = jnp.float32
+    sends = send_cells.reshape(-1)
+    slots = sends.shape[0]
+    rows = 2 * RIM_CELLS + cells + slots
     near = neighbours.reshape(-1)
-    density, pressure = densities(near, counts, table, cell_count)
-    q_table = full_table(pressure, chosen, present)
+    dma = pltpu.SemaphoreType.DMA
+    sems = [dma((peer_count,)), dma((peer_count,)), dma((4,))]
+
+    capacity = max(2, cells // (2 * peer_count))
+    everyone = owners[0]
+    mine = lax.dynamic_slice_in_dim(everyone, me * cells, cells)
+    index = jnp.arange(cells, dtype=jnp.int32)
+    earlier = (mine[None, :] == mine[:, None]) & (index[None, :] < index[:, None])
+    key = mine * cells + jnp.sum(earlier.astype(jnp.int32), 1)
+    slot = jnp.arange(peer_count * capacity, dtype=jnp.int32)
+    wanted = slot // capacity * cells + slot % capacity
+    picks = jnp.sum(jnp.where(key[None, :] == wanted[:, None], index[None, :], 0), 1)
+    comes = everyone.reshape(peer_count, cells) == me
+    rank = jnp.sum(
+        (comes[:, None, :] & (index[None, None, :] < index[None, :, None])).astype(jnp.int32), 2
+    )
+    amounts = jnp.sum(comes.astype(jnp.int32), 1)
+    device = jnp.arange(peer_count, dtype=jnp.int32)
+    starts = jnp.sum(jnp.where(device[None, :] < device[:, None], amounts[None, :], 0), 1)
+    code = jnp.where(
+        (device == me)[:, None], index[None, :], cells + device[:, None] * capacity + rank
+    )
+    goal = jnp.where(comes, starts[:, None] + rank, -1)
+    order = jnp.sum(
+        jnp.where(goal.reshape(1, -1) == index[:, None], code.reshape(1, -1), 0), 1
+    )
+
+    table = remote(
+        fields_kernel,
+        1,
+        smem(2) + vmem(4),
+        jax.ShapeDtypeStruct((rows, 8, width), f32),
+        [pltpu.VMEM((slots, 8, width), f32)] + sems,
+    )(counts, sends, positions, velocities, masses, walls)
+    density, pressure = densities(near, counts, table, cells)
+    q_table = remote(
+        pressure_kernel,
+        2,
+        smem(1) + vmem(1),
+        jax.ShapeDtypeStruct((rows, 1, width), f32),
+        [pltpu.VMEM((slots, 1, width), f32)] + sems,
+    )(sends, pressure)
     moved = forces(near, counts, table, q_table, walls, density)
-    capacity = max(2, cell_count // (2 * peer_count))
-    own_index = lax.axis_index("dev")
-    group_owner = owners[0]
-    own_owners = lax.dynamic_slice_in_dim(group_owner, own_index * cell_count, cell_count)
-    one_hot = (own_owners[:, None] == jnp.arange(peer_count, dtype=jnp.int32)[None, :]).astype(
-        jnp.int32
-    )
-    send_rank = jnp.sum((jnp.cumsum(one_hot, 0) - one_hot) * one_hot, 1)
-    staying = own_owners == own_index
-    slot_index = jnp.where(staying, peer_count * capacity, own_owners * capacity + send_rank)
-    outbox = (
-        jnp.zeros((peer_count * capacity, 8, block_width), jnp.float32)
-        .at[slot_index]
-        .set(moved, mode="drop")
-    )
-    inbox = lax.all_to_all(outbox, "dev", split_axis=0, concat_axis=0, tiled=True)
-    arrivals = jnp.sum(
-        (group_owner.reshape(peer_count, cell_count) == own_index).astype(jnp.int32), 1
-    )
-    arrival_start = jnp.cumsum(arrivals) - arrivals
-    rank_in = lax.broadcasted_iota(jnp.int32, (peer_count, capacity), 1)
-    source_row = lax.broadcasted_iota(jnp.int32, (peer_count, capacity), 0)
-    usable = (rank_in < arrivals[:, None]) & (source_row != own_index)
-    arrival_slot = jnp.where(usable, arrival_start[:, None] + rank_in, cell_count).reshape(-1)
-    keep_slot = jnp.where(staying, arrival_start[own_index] + send_rank, cell_count)
-    settled = jnp.zeros((cell_count, 8, block_width), jnp.float32)
-    settled = settled.at[arrival_slot].set(inbox, mode="drop")
-    settled = settled.at[keep_slot].set(moved, mode="drop")
-    settled = jnp.transpose(settled, (1, 0, 2))
-    return (settled[0:6], settled[6])
+    return remote(
+        settle_kernel,
+        3,
+        smem(2) + vmem(1),
+        (jax.ShapeDtypeStruct((6, cells, width), f32), jax.ShapeDtypeStruct((cells, width), f32)),
+        [
+            pltpu.VMEM((peer_count * capacity, 8, width), f32),
+            pltpu.VMEM((cells + peer_count * capacity, 8, width), f32),
+        ]
+        + sems[:2],
+    )(picks, order, moved)
 
 
 def solution(mesh):

time: 114 us -> 87.4 us (0.77)
  starting transfers between devices: 23.2 us -> 0 us
  Pallas kernels: 58.5 us -> 79.7 us
  waiting for transfers between devices: 10.4 us -> 0 us
  local copies, waits for them, and re-layouts: 15.2 us -> 5.55 us
  other arithmetic: 4.63 us -> 1.13 us
    pallas_call x0 -> x3, Pallas kernels: none -> 21.1 us  [the longest x1 8.93 us: shards(): remote(fields_kernel, 1, smem(2) + vmem(4), jax.ShapeDtypeStruct((rows, 8...]
    all_to_all x3 -> x0, starting transfers between devices: 13.7 us -> none  [the longest x2 9.4 us: full_table(): lax.all_to_all(out, 'dev', split_axis=0, concat_axis=0, tiled=True)]
    ppermute x4 -> x0, starting transfers between devices: 9.54 us -> none  [the longest x2 6.95 us: full_table(): lax.ppermute(cells[-RIM_CELLS:], 'group', [(i, i + 1) for i in range(coun...]
    scatter x3 -> x0, local copies, waits for them, and re-layouts: 6.87 us -> none  [the longest x1 4.32 us: shards(): outbox = jnp.zeros((peer_count * capacity, 8, block_width), jnp.float32)....]
    all_to_all x3 -> x0, waiting for transfers between devices: 5.5 us -> none  [the longest x1 5.49 us: shards(): lax.all_to_all(outbox, 'dev', split_axis=0, concat_axis=0, tiled=True)]
    ppermute x4 -> x0, waiting for transfers between devices: 4.93 us -> none  [the longest x2 4.93 us: full_table(): lax.ppermute(cells[:RIM_CELLS], 'group', [(i + 1, i) for i in range(count...]
    mul x2 -> x0, other arithmetic: 1.42 us -> none  [full_table(): out = cells[chosen] * present.reshape((-1,) + (1,) * (cells.ndim - 1))]
    gather x3 -> x0, local copies, waits for them, and re-layouts: 1.16 us -> none  [full_table(): out = cells[chosen] * present.reshape((-1,) + (1,) * (cells.ndim - 1))]
  transfers between devices with their start and end apart: 7 -> 0, of which waited for: 3 -> 0; matrix products, arithmetic and copies ran while one was open for 2% -> 0% of each run, Pallas kernels for 0% -> 0%
where the time goes in v2:
time: 87.4 us; the launch traced here: 87.1 us
  Pallas kernels  79.7 us (91%)
  local copies, waits for them, and re-layouts  5.55 us (6%)
  other arithmetic  1.13 us (1%)
    pallas_call x1, Pallas kernels, forces(): pl.pallas_call(force_kernel, out_shape=jax.ShapeDtypeStruct((rho.shape[0]...  41 us
    pallas_call x1, Pallas kernels, densities(): pl.pallas_call(density_kernel, out_shape=(shape, shape), in_specs=smem(2)...  17.6 us
    pallas_call x1, Pallas kernels, shards(): remote(fields_kernel, 1, smem(2) + vmem(4), jax.ShapeDtypeStruct((rows, 8...  8.93 us
    pallas_call x1, Pallas kernels, shards(): remote(settle_kernel, 3, smem(2) + vmem(1), (jax.ShapeDtypeStruct((6, cel...  6.18 us
    pallas_call x1, Pallas kernels, shards(): remote(pressure_kernel, 2, smem(1) + vmem(1), jax.ShapeDtypeStruct((rows,...  6.03 us
    unnamed x20, local copies, waits for them, and re-layouts  5.05 us

profile of v2, /device:TPU:0, one launch (start us, length us, event | category | flops | bytes accessed | tf_op | source)
XLA Modules:
  0.0 87.1 jit_solution(3925570314173687008)
XLA Ops:
  0.6 0.7 copy-done.5
  1.4 0.2 convert_reduce_fusion.1
  1.7 0.1 eq.85
  1.8 0.1 convert_reduce_fusion.2
  1.9 0.1 select_reduce_fusion.2
  2.0 0.2 select_reduce_fusion.1.picks
  2.2 0.5 copy-done.7
  2.7 0.1 copy.15
  2.8 0.1 reshape.121.sends
  2.9 0.2 convert_reduce_fusion
  3.4 0.1 select_reduce_fusion.order
  3.6 0.1 copy.14
  3.7 0.1 reshape.120.near
  3.8 0.1 copy-done
  3.9 0.4 copy-done.4
  4.3 0.9 %copy-done.1 = f32[3,32,256]{2,1,0:T(8,128)S(1)} copy-done((f32[3,32,256]{2,1,0:T(8,128)S(1)}, f32[3,32,256]{2,1,0:T(8,128)}, u32[]{:S(2)}) %copy-start.1) | copy-done | bytes 98328
  5.2 0.9 %copy-done.2 = f32[3,32,256]{2,1,0:T(8,128)S(1)} copy-done((f32[3,32,256]{2,1,0:T(8,128)S(1)}, f32[3,32,256]{2,1,0:T(8,128)}, u32[]{:S(2)}) %copy-start.2) | copy-done | bytes 98328
  6.1 8.9 %shard_map.95.table = f32[56,8,256]{2,1,0:T(8,128)S(1)} custom-call(s32[32]{0:T(128)S(1)} %copy-done.4, s32[16]{0:T(128)S(1)} %reshape.121.sends, f32[3,32,256]{2,1,0:T(8,128)S(1)} %copy-done.1, f32[3,32,256]{2,1,0:T(8,128)S(1)} %copy-done.2, f32[32,256]{1,0:T(8,128)S(1)} %copy-done.3, s32[32,256]{1,0:T(8,128)S(1)} %copy-done), custom_call_target="tpu_custom_call" | custom-call | tf_op jit(solution)/shard_map/pallas_call | solution.py:444
  15.0 17.6 %shard_map.96 = (f32[32,1,256]{2,1,0:T(1,128)S(1)}, f32[32,1,256]{2,1,0:T(1,128)S(1)}) custom-call(s32[96]{0:T(128)S(1)} %reshape.120.near, s32[32]{0:T(128)S(1)} %copy-done.4, f32[56,8,256]{2,1,0:T(8,128)S(1)} %shard_map.95.table), custom_call_target="tpu_custom_call" | custom-call | tf_op jit(solution)/shard_map/pallas_call | solution.py:370
  32.6 6.0 %shard_map.97.q_table = f32[56,1,256]{2,1,0:T(1,128)S(1)} custom-call(s32[16]{0:T(128)S(1)} %reshape.121.sends, f32[32,1,256]{2,1,0:T(1,128)S(1)} %get-tuple-element.4.pressure), custom_call_target="tpu_custom_call" | custom-call | tf_op jit(solution)/shard_map/pallas_call | solution.py:452
  38.7 41.0 %shard_map.98.moved = f32[32,8,256]{2,1,0:T(8,128)S(1)} custom-call(s32[96]{0:T(128)S(1)} %reshape.120.near, s32[32]{0:T(128)S(1)} %copy-done.4, f32[56,8,256]{2,1,0:T(8,128)S(1)} %shard_map.95.table, f32[56,1,256]{2,1,0:T(1,128)S(1)} %shard_map.97.q_table, s32[32,256]{1,0:T(8,128)S(1)} %copy-done, f32[32,1,256]{2,1,0:T(1,128)S(1)} %get-tuple-element.5.rho_ref), custom_call_target="tpu_custom_call" | custom-call | tf_op jit(solution)/shard_map/pallas_call | solution.py:382
  79.6 6.2 %shard_map.99 = (f32[6,32,256]{2,1,0:T(8,128)S(1)}, f32[32,256]{1,0:T(8,128)S(1)}) custom-call(s32[16]{0:T(128)S(1)} %select_reduce_fusion.1.picks, s32[32]{0:T(128)S(1)} %select_reduce_fusion.order, f32[32,8,256]{2,1,0:T(8,128)S(1)} %shard_map.98.moved), custom_call_target="tpu_custom_call" | custom-call | tf_op jit(solution)/shard_map/pallas_call | solution.py:460
  85.8 0.7 copy.18
  86.5 0.6 copy.19
  (21 shorter events, 0.5 us)
Async XLA Ops:
  0.6 0.7 copy-start.5
  2.0 0.7 copy-start.7
  2.9 0.7 copy-start.6
  3.1 0.8 copy-start
  3.1 0.8 copy-start.3
  3.7 0.7 copy-start.4
  4.3 0.9 %copy-start.1 = (f32[3,32,256]{2,1,0:T(8,128)S(1)}, f32[3,32,256]{2,1,0:T(8,128)}, u32[]{:S(2)}) copy-start(f32[3,32,256]{2,1,0:T(8,128)} %pos.1) | copy-start | bytes 294916
  5.2 0.9 %copy-start.2 = (f32[3,32,256]{2,1,0:T(8,128)S(1)}, f32[3,32,256]{2,1,0:T(8,128)}, u32[]{:S(2)}) copy-start(f32[3,32,256]{2,1,0:T(8,128)} %vel.1) | copy-start | bytes 294916

commit v3 on v2

--- a/solution.py
+++ b/solution.py
@@ -56,9 +56,55 @@
     return jnp.dot(a, b, preferred_element_type=jnp.float32)
 
 
-def partner_rows(near, c):
-    near_cells = 3
-    return [RIM_CELLS + c] + [near[c * near_cells + k] for k in range(near_cells)]
+HALF = 128
+NEAR = 3
+CLASSES = [(width, n) for width in (1, 2) for n in range(NEAR + width, 2 * NEAR + width + 1)]
+
+
+def sort_cells(near, filled, lists, sizes, extra):
+    cells = near.shape[0] // NEAR
+    base = 2 * (NEAR + 1)
+    for k in range(base * 2):
+        sizes[k] = 0
+
+    def one(c, _):
+        own = filled[RIM_CELLS + c]
+        count = 0
+        for r in [RIM_CELLS + c] + [near[c * NEAR + k] for k in range(NEAR)]:
+            extra[c * 4 + count] = r
+            count = count + filled[r]
+        cls = own * (NEAR + 1) + count - own
+        size = sizes[cls]
+        lists[cls * cells + size] = c
+        sizes[cls] = size + 1
+        return 0
+
+    lax.fori_loop(0, cells, one, 0)
+
+
+def by_class(lists, sizes, body, together):
+    cells = lists.shape[0] // len(CLASSES)
+    for cls, (width, n) in enumerate(CLASSES):
+        size = sizes[cls]
+
+        def step(k, _, cls=cls, width=width, n=n, size=size):
+            for u in range(together):
+                at = jnp.minimum(k * together + u, size - 1)
+                body(lists[cls * cells + at], width * HALF, n)
+            return 0
+
+        lax.fori_loop(0, (size + together - 1) // together, step, 0)
+
+
+def chunks(near, extra, c, n):
+    rows = [RIM_CELLS + c] + [near[c * NEAR + k] for k in range(NEAR)]
+    return [2 * r for r in rows] + [2 * extra[c * 4 + k] + 1 for k in range(n - NEAR - 1)]
+
+
+def widen(row, width):
+    if row.shape[1] == width:
+        return row
+    return jnp.concatenate([row, jnp.zeros((row.shape[0], width - row.shape[1]), row.dtype)], 1)
 
 
 def to_peers(act):
@@ -265,78 +311,88 @@
     lax.fori_loop(0, cells, place, 0)
 
 
-def density_kernel(near, counts, table, rho_ref, q_ref, left):
+def density_kernel(near, counts, filled, table, rho_ref, q_ref, lists, sizes, extra, left):
     rows_total = table.shape[0]
-    cells = rho_ref.shape[0]
+    full = table.shape[2]
+    sort_cells(near, filled, lists, sizes, extra)
 
     def prepare(r, _):
         row = table[r]
         mass = row[3:4]
         root = jnp.where(mass > 0.0, jnp.exp(jnp.log(jnp.maximum(mass, 1e-30)) * (1.0 / 3.0)), 0.0)
-        left[r] = source_side(row[0:3], root)
-        return 0
-
-    lax.fori_loop(0, rows_total, prepare, 0)
-
-    def cell(c, _):
-        right = target_side(table[RIM_CELLS + c][0:3])
-        total = jnp.zeros((8, right.shape[1]), jnp.float32)
-        for r in partner_rows(near, c):
-            u = jnp.maximum(mm(left[r], right), 0.0)
-            total = total + jnp.sum((u * u * u).reshape(-1, 8, u.shape[1]), axis=0)
+        side = source_side(row[0:3], root)
+        left[2 * r] = side[:HALF]
+        left[2 * r + 1] = side[HALF:]
+        return 0
+
+    lax.fori_loop(0, rows_total, prepare, 0, unroll=8)
+
+    def cell(c, width, n):
+        right = target_side(table[RIM_CELLS + c][0:3, :width])
+        total = jnp.zeros((8, width), jnp.float32)
+        for k in chunks(near, extra, c, n):
+            u = jnp.maximum(mm(left[k], right), 0.0)
+            total = total + jnp.sum((u * u * u).reshape(-1, 8, width), axis=0)
         rho = jnp.sum(total, axis=0, keepdims=True)
         slot = lax.broadcasted_iota(jnp.int32, rho.shape, 1)
         active = (slot < counts[c]).astype(jnp.float32)
         safe = active * rho + (1.0 - active)
-        rho_ref[c] = rho
-        q_ref[c] = active * STIFFNESS * (rho - REST_DENSITY) / (safe * safe)
-        return 0
-
-    lax.fori_loop(0, cells, cell, 0)
-
-
-def force_kernel(near, counts, table, q_table, walls, rho_ref, out_ref, left, red1, red2, red3):
+        rho_ref[c] = widen(rho, full)
+        q_ref[c] = widen(active * STIFFNESS * (rho - REST_DENSITY) / (safe * safe), full)
+
+    by_class(lists, sizes, cell, 2)
+
+
+def force_kernel(
+    near, counts, lists, sizes, extra, table, q_table, walls, rho_ref, out_ref, left, red1, red2, red3
+):
     rows_total = table.shape[0]
-    cells = rho_ref.shape[0]
+    full = table.shape[2]
 
     def prepare(r, _):
         row = table[r]
         pos, mass, vel, bond = row[0:3], row[3:4], row[4:7], row[7:8]
-        left[r] = source_side(pos, jnp.ones_like(mass))
+        side = source_side(pos, jnp.ones_like(mass))
         mq = mass * q_table[r]
         two = jnp.concatenate([mass, mass * pos, mq, mq * pos], 0)
         one = jnp.concatenate([bond, bond * pos, mass, mass * vel], 0)
         h2 = coarse(two)
         h1 = coarse(one)
         l1 = one - h1
-        red2[r] = jnp.concatenate([h2, two - h2], 0).astype(jnp.bfloat16)
-        red1[r] = jnp.concatenate([h1[0:4], l1[0:4], l1[0:4] * 0.0, l1[0:4] * 0.0], 0).astype(jnp.bfloat16)
-        red3[r] = jnp.concatenate([h1[4:8], l1[4:8], l1[0:4] * 0.0, l1[0:4] * 0.0], 0).astype(jnp.bfloat16)
-        return 0
-
-    lax.fori_loop(0, rows_total, prepare, 0)
-
-    def cell(c, _):
-        row = table[RIM_CELLS + c]
+        none = jnp.zeros_like(one)
+        r2 = jnp.concatenate([h2, two - h2], 0).astype(jnp.bfloat16)
+        r1 = jnp.concatenate([h1[0:4], l1[0:4], none], 0).astype(jnp.bfloat16)
+        r3 = jnp.concatenate([h1[4:8], l1[4:8], none], 0).astype(jnp.bfloat16)
+        for k in range(2):
+            part = slice(k * HALF, (k + 1) * HALF)
+            left[2 * r + k] = side[part]
+            red1[2 * r + k] = r1[:, part]
+            red2[2 * r + k] = r2[:, part]
+            red3[2 * r + k] = r3[:, part]
+        return 0
+
+    lax.fori_loop(0, rows_total, prepare, 0, unroll=8)
+
+    def cell(c, width, n):
+        row = table[RIM_CELLS + c][:, :width]
         pos, vel = row[0:3], row[4:7]
         right = target_side(pos)
-        width = right.shape[1]
         s1 = jnp.zeros((16, width), jnp.float32)
         s2 = jnp.zeros((16, width), jnp.float32)
         s3 = jnp.zeros((16, width), jnp.float32)
-        for r in partner_rows(near, c):
-            w = jnp.maximum(mm(left[r], right), 0.0)
+        for k in chunks(near, extra, c, n):
+            w = jnp.maximum(mm(left[k], right), 0.0)
             w2 = w * w
             w3 = w2 * w
             high = w2.astype(jnp.bfloat16)
             low = (w2 - high.astype(jnp.float32)).astype(jnp.bfloat16)
-            s2 = s2 + mm(red2[r], high) + mm(red2[r], low)
-            s1 = s1 + mm(red1[r], w.astype(jnp.bfloat16))
-            s3 = s3 + mm(red3[r], w3.astype(jnp.bfloat16))
+            s2 = s2 + mm(red2[k], high) + mm(red2[k], low)
+            s1 = s1 + mm(red1[k], w.astype(jnp.bfloat16))
+            s3 = s3 + mm(red3[k], w3.astype(jnp.bfloat16))
         s2 = s2[0:8] + s2[8:16]
         s1 = s1[0:4] + s1[4:8]
         s3 = s3[0:4] + s3[4:8]
-        q = q_table[RIM_CELLS + c]
+        q = q_table[RIM_CELLS + c][:, :width]
         acc = (
             (6.0 / SUPPORT) * (q * (pos * s2[0:1] - s2[1:4]) + (pos * s2[4:5] - s2[5:8]))
             - (pos * s1[0:1] - s1[1:4])
@@ -346,14 +402,15 @@
         acc = acc - jnp.where(component == 2, GRAVITY, 0.0)
         slot = lax.broadcasted_iota(jnp.int32, q.shape, 1)
         active = (slot < counts[c]).astype(jnp.float32)
-        fluid = active - walls[pl.ds(c, 1)].astype(jnp.float32) * active
+        fluid = active - walls[pl.ds(c, 1)][:, :width].astype(jnp.float32) * active
         new_vel = vel + TIME_STEP * fluid * acc
         new_pos = pos + TIME_STEP * fluid * new_vel
-        rho = rho_ref[c]
-        out_ref[c] = active * jnp.concatenate([new_pos, new_vel, rho, jnp.zeros_like(rho)], 0)
-        return 0
-
-    lax.fori_loop(0, cells, cell, 0)
+        rho = rho_ref[c][:, :width]
+        out_ref[c] = widen(
+            active * jnp.concatenate([new_pos, new_vel, rho, jnp.zeros_like(rho)], 0), full
+        )
+
+    by_class(lists, sizes, cell, 1)
 
 
 def vmem(count):
@@ -364,30 +421,31 @@
     return [pl.BlockSpec(memory_space=pltpu.SMEM)] * count
 
 
-def densities(near, counts, table, cells):
+def densities(near, counts, filled, table, cells):
     rows, _, width = table.shape
     shape = jax.ShapeDtypeStruct((cells, 1, width), jnp.float32)
+    plan = [(len(CLASSES) * cells,), (4 * (NEAR + 1),), (4 * cells,)]
     return pl.pallas_call(
         density_kernel,
-        out_shape=(shape, shape),
-        in_specs=smem(2) + vmem(1),
-        out_specs=tuple(vmem(2)),
-        scratch_shapes=[pltpu.VMEM((rows, width, 48), jnp.bfloat16)],
+        out_shape=(shape, shape) + tuple(jax.ShapeDtypeStruct(p, jnp.int32) for p in plan),
+        in_specs=smem(3) + vmem(1),
+        out_specs=tuple(vmem(2) + smem(3)),
+        scratch_shapes=[pltpu.VMEM((rows * 2, HALF, 48), jnp.bfloat16)],
         compiler_params=pltpu.CompilerParams(vmem_limit_bytes=48 * 2**20),
-    )(near, counts, table)
-
-
-def forces(near, counts, table, q_table, walls, rho):
+    )(near, counts, filled, table)
+
+
+def forces(near, counts, plan, table, q_table, walls, rho):
     rows, _, width = table.shape
     return pl.pallas_call(
         force_kernel,
         out_shape=jax.ShapeDtypeStruct((rho.shape[0], 8, width), jnp.float32),
-        in_specs=smem(2) + vmem(4),
+        in_specs=smem(5) + vmem(4),
         out_specs=vmem(1)[0],
-        scratch_shapes=[pltpu.VMEM((rows, width, 48), jnp.bfloat16)]
-        + [pltpu.VMEM((rows, 16, width), jnp.bfloat16)] * 3,
+        scratch_shapes=[pltpu.VMEM((rows * 2, HALF, 48), jnp.bfloat16)]
+        + [pltpu.VMEM((rows * 2, 16, HALF), jnp.bfloat16)] * 3,
         compiler_params=pltpu.CompilerParams(vmem_limit_bytes=48 * 2**20),
-    )(near, counts, table, q_table, walls, rho)
+    )(near, counts, *plan, table, q_table, walls, rho)
 
 
 def remote(kernel, collective_id, in_specs, out_shape, scratch):
@@ -448,7 +506,8 @@
         jax.ShapeDtypeStruct((rows, 8, width), f32),
         [pltpu.VMEM((slots, 8, width), f32)] + sems,
     )(counts, sends, positions, velocities, masses, walls)
-    density, pressure = densities(near, counts, table, cells)
+    filled = jnp.any(table[:, 3, HALF:] != 0.0, axis=1).astype(jnp.int32)
+    density, pressure, *plan = densities(near, counts, filled, table, cells)
     q_table = remote(
         pressure_kernel,
         2,
@@ -456,7 +515,7 @@
         jax.ShapeDtypeStruct((rows, 1, width), f32),
         [pltpu.VMEM((slots, 1, width), f32)] + sems,
     )(sends, pressure)
-    moved = forces(near, counts, table, q_table, walls, density)
+    moved = forces(near, counts, plan, table, q_table, walls, density)
     return remote(
         settle_kernel,
         3,

time: 87.4 us -> 87.2 us (level); the launches traced: 87.1 us -> 86 us
  Pallas kernels: 79.7 us -> 75.8 us
  local copies, waits for them, and re-layouts: 5.55 us -> 7.2 us
  other arithmetic: 1.13 us -> 2.23 us
    pallas_call x1, Pallas kernels: 17.6 us -> 9.61 us  [densities(): pl.pallas_call(density_kernel, out_shape=(shape, shape) + tuple((jax.Shap...]
    pallas_call x1, Pallas kernels: 6.18 us -> 13.7 us  [shards(): remote(settle_kernel, 3, smem(2) + vmem(1), (jax.ShapeDtypeStruct((6, cel...]
    pallas_call x1, Pallas kernels: 41 us -> 36.5 us  [forces(): pl.pallas_call(force_kernel, out_shape=jax.ShapeDtypeStruct((rho.shape[0]...]
    unnamed x20, local copies, waits for them, and re-layouts: 5.05 us -> 6.7 us
    reduce_or x0 -> x1, other arithmetic: none -> 1.08 us  [shards(): filled = jnp.any(table[:, 3, HALF:] != 0.0, axis=1).astype(jnp.int32)]
    pallas_call x1, Pallas kernels: 6.03 us -> 7.1 us  [shards(): remote(pressure_kernel, 2, smem(1) + vmem(1), jax.ShapeDtypeStruct((rows,...]
where the time goes in v3:
time: 87.2 us; the launch traced here: 86 us
  Pallas kernels  75.8 us (87%)
  local copies, waits for them, and re-layouts  7.2 us (8%)
  other arithmetic  2.23 us (3%)
    pallas_call x1, Pallas kernels, forces(): pl.pallas_call(force_kernel, out_shape=jax.ShapeDtypeStruct((rho.shape[0]...  36.5 us
    pallas_call x1, Pallas kernels, shards(): remote(settle_kernel, 3, smem(2) + vmem(1), (jax.ShapeDtypeStruct((6, cel...  13.7 us
    pallas_call x1, Pallas kernels, densities(): pl.pallas_call(density_kernel, out_shape=(shape, shape) + tuple((jax.Shap...  9.61 us
    pallas_call x1, Pallas kernels, shards(): remote(fields_kernel, 1, smem(2) + vmem(4), jax.ShapeDtypeStruct((rows, 8...  8.93 us
    pallas_call x1, Pallas kernels, shards(): remote(pressure_kernel, 2, smem(1) + vmem(1), jax.ShapeDtypeStruct((rows,...  7.1 us
    unnamed x20, local copies, waits for them, and re-layouts  6.7 us

profile of v3, /device:TPU:0, one launch (start us, length us, event | category | flops | bytes accessed | tf_op | source)
XLA Modules:
  0.0 86.0 jit_solution(18155236974485885502)
XLA Ops:
  0.6 0.8 copy.15
  1.5 0.6 copy-done.5
  2.0 0.8 copy-done
  2.8 0.9 %copy-done.2 = f32[3,32,256]{2,1,0:T(8,128)S(1)} copy-done((f32[3,32,256]{2,1,0:T(8,128)S(1)}, f32[3,32,256]{2,1,0:T(8,128)}, u32[]{:S(2)}) %copy-start.2) | copy-done | bytes 98328
  3.7 0.9 %copy-done.3 = f32[3,32,256]{2,1,0:T(8,128)S(1)} copy-done((f32[3,32,256]{2,1,0:T(8,128)S(1)}, f32[3,32,256]{2,1,0:T(8,128)}, u32[]{:S(2)}) %copy-start.3) | copy-done | bytes 98328
  4.6 0.8 copy-done.4
  5.3 8.9 %shard_map.95.table = f32[56,8,256]{2,1,0:T(8,128)S(1)} custom-call(s32[32]{0:T(128)S(1)} %copy-done.5, s32[16]{0:T(128)S(1)} %reshape.123.sends, f32[3,32,256]{2,1,0:T(8,128)S(1)} %copy-done.2, f32[3,32,256]{2,1,0:T(8,128)S(1)} %copy-done.3, f32[32,256]{1,0:T(8,128)S(1)} %copy-done.4, s32[32,256]{1,0:T(8,128)S(1)} %copy-done), custom_call_target="tpu_custom_call" | custom-call | tf_op jit(solution)/shard_map/pallas_call | solution.py:502
  14.3 1.1 %compare_reduce_fusion = pred[56]{0:T(512)(128)(4,1)S(1)} fusion(f32[56,8,256]{2,1,0:T(8,128)S(1)} %shard_map.95.table), kind=kLoop, calls=%fused_computation.1 | loop fusion | flops 14280 | bytes 28728 | tf_op jit(solution)/shard_map/reduce_or | solution.py:509
  15.4 0.1 copy.14
  15.5 0.1 reshape.122.near
  15.6 9.6 %shard_map.96 = (f32[32,1,256]{2,1,0:T(1,128)S(1)}, f32[32,1,256]{2,1,0:T(1,128)S(1)}, s32[256]{0:T(256)S(1)}, s32[16]{0:T(128)S(1)}, s32[128]{0:T(128)S(1)}) custom-call(s32[96]{0:T(128)S(1)} %reshape.122.near, s32[32]{0:T(128)S(1)} %copy-done.5, s32[56]{0:T(128)S(1)} %convert_element_type.19.filled, f32[56,8,256]{2,1,0:T(8,128)S(1)} %shard_map.95.table), custom_call_target="tpu_custom_call" | custom-call | tf_op jit(solution)/shard_map/pallas_call | solution.py:428
  25.2 7.1 %shard_map.97.q_table = f32[56,1,256]{2,1,0:T(1,128)S(1)} custom-call(s32[16]{0:T(128)S(1)} %reshape.123.sends, f32[32,1,256]{2,1,0:T(1,128)S(1)} %get-tuple-element.10.pressure), custom_call_target="tpu_custom_call" | custom-call | tf_op jit(solution)/shard_map/pallas_call | solution.py:511
  32.3 36.5 %shard_map.98.moved = f32[32,8,256]{2,1,0:T(8,128)S(1)} custom-call(s32[96]{0:T(128)S(1)} %reshape.122.near, s32[32]{0:T(128)S(1)} %copy-done.5, s32[256]{0:T(256)S(1)} %get-tuple-element.7.lists, s32[16]{0:T(128)S(1)} %get-tuple-element.8.sizes, s32[128]{0:T(128)S(1)} %get-tuple-element.9.extra, f32[56,8,256]{2,1,0:T(8,128)S(1)} %shard_map.95.table, ...), custom_call_target="tpu_custom_call" | custom-call | tf_op jit(solution)/shard_map/pallas_call | solution.py:440
  68.8 0.7 copy-done.6
  69.6 0.2 convert_reduce_fusion.1
  69.8 0.2 select_reduce_fusion.1.picks
  70.0 0.1 eq.85
  70.1 0.2 convert_reduce_fusion
  70.4 0.1 convert_reduce_fusion.2
  70.5 0.1 select_reduce_fusion.2
  70.9 0.1 select_reduce_fusion.order
  71.0 13.7 %shard_map.99 = (f32[6,32,256]{2,1,0:T(8,128)S(1)}, f32[32,256]{1,0:T(8,128)S(1)}) custom-call(s32[16]{0:T(128)S(1)} %select_reduce_fusion.1.picks, s32[32]{0:T(128)S(1)} %select_reduce_fusion.order, f32[32,8,256]{2,1,0:T(8,128)S(1)} %shard_map.98.moved), custom_call_target="tpu_custom_call" | custom-call | tf_op jit(solution)/shard_map/pallas_call | solution.py:519
  84.7 0.7 copy.18
  85.3 0.6 copy.19
  (23 shorter events, 0.5 us)
Async XLA Ops:
  1.4 0.7 copy-start.5
  2.0 0.8 copy-start
  2.8 0.9 %copy-start.2 = (f32[3,32,256]{2,1,0:T(8,128)S(1)}, f32[3,32,256]{2,1,0:T(8,128)}, u32[]{:S(2)}) copy-start(f32[3,32,256]{2,1,0:T(8,128)} %pos.1) | copy-start | bytes 294916
  3.7 0.9 %copy-start.3 = (f32[3,32,256]{2,1,0:T(8,128)S(1)}, f32[3,32,256]{2,1,0:T(8,128)}, u32[]{:S(2)}) copy-start(f32[3,32,256]{2,1,0:T(8,128)} %vel.1) | copy-start | bytes 294916
  4.6 0.8 copy-start.4
  14.3 1.1 %copy-start.7 = (s32[32,3]{0,1:T(4,128)S(1)}, s32[32,3]{0,1:T(4,128)}, u32[]{:S(2)}) copy-start(s32[32,3]{0,1:T(4,128)} %param.13) | copy-start | bytes 1156
  25.2 7.1 %copy-start.1 = (s32[32,256]{1,0:T(8,128)S(1)}, s32[32,256]{1,0:T(8,128)}, u32[]{:S(2)}) copy-start(s32[32,256]{1,0:T(8,128)} %walls.3) | copy-start | bytes 98308
  68.8 0.7 copy-start.6

commit v4 on v3

--- a/solution.py
+++ b/solution.py
@@ -344,7 +344,7 @@
 
 
 def force_kernel(
-    near, counts, lists, sizes, extra, table, q_table, walls, rho_ref, out_ref, left, red1, red2, red3
+    near, counts, lists, sizes, extra, table, q_table, walls, rho_ref, out_ref, left, red_a, red_b
 ):
     rows_total = table.shape[0]
     full = table.shape[2]
@@ -359,16 +359,17 @@
         h2 = coarse(two)
         h1 = coarse(one)
         l1 = one - h1
-        none = jnp.zeros_like(one)
-        r2 = jnp.concatenate([h2, two - h2], 0).astype(jnp.bfloat16)
-        r1 = jnp.concatenate([h1[0:4], l1[0:4], none], 0).astype(jnp.bfloat16)
-        r3 = jnp.concatenate([h1[4:8], l1[4:8], none], 0).astype(jnp.bfloat16)
+        r2 = jnp.concatenate([h2, two - h2], 0)
+        r1 = jnp.concatenate([h1[0:4], l1[0:4]], 0)
+        r3 = jnp.concatenate([h1[4:8], l1[4:8]], 0)
+        none = jnp.zeros((8, HALF), jnp.float32)
         for k in range(2):
             part = slice(k * HALF, (k + 1) * HALF)
             left[2 * r + k] = side[part]
-            red1[2 * r + k] = r1[:, part]
-            red2[2 * r + k] = r2[:, part]
-            red3[2 * r + k] = r3[:, part]
+            red_a[2 * r + k] = jnp.concatenate([r2[:, part]] * 2, 1).astype(jnp.bfloat16)
+            red_b[2 * r + k] = jnp.concatenate(
+                [jnp.concatenate([r1[:, part], none], 1), jnp.concatenate([none, r3[:, part]], 1)], 0
+            ).astype(jnp.bfloat16)
         return 0
 
     lax.fori_loop(0, rows_total, prepare, 0, unroll=8)
@@ -377,18 +378,26 @@
         row = table[RIM_CELLS + c][:, :width]
         pos, vel = row[0:3], row[4:7]
         right = target_side(pos)
-        s1 = jnp.zeros((16, width), jnp.float32)
         s2 = jnp.zeros((16, width), jnp.float32)
-        s3 = jnp.zeros((16, width), jnp.float32)
+        s13 = jnp.zeros((16, width), jnp.float32)
         for k in chunks(near, extra, c, n):
             w = jnp.maximum(mm(left[k], right), 0.0)
             w2 = w * w
             w3 = w2 * w
             high = w2.astype(jnp.bfloat16)
             low = (w2 - high.astype(jnp.float32)).astype(jnp.bfloat16)
-            s2 = s2 + mm(red2[k], high) + mm(red2[k], low)
-            s1 = s1 + mm(red1[k], w.astype(jnp.bfloat16))
-            s3 = s3 + mm(red3[k], w3.astype(jnp.bfloat16))
+            pair_a = jnp.concatenate([high, low], 0)
+            pair_b = jnp.concatenate([w.astype(jnp.bfloat16), w3.astype(jnp.bfloat16)], 0)
+            if width == HALF:
+                both = mm(
+                    jnp.concatenate([red_a[k], red_b[k]], 0), jnp.concatenate([pair_a, pair_b], 1)
+                )
+                s2 = s2 + both[:16, :HALF]
+                s13 = s13 + both[16:, HALF:]
+            else:
+                s2 = s2 + mm(red_a[k], pair_a)
+                s13 = s13 + mm(red_b[k], pair_b)
+        s1, s3 = s13[0:8], s13[8:16]
         s2 = s2[0:8] + s2[8:16]
         s1 = s1[0:4] + s1[4:8]
         s3 = s3[0:4] + s3[4:8]
@@ -443,7 +452,7 @@
         in_specs=smem(5) + vmem(4),
         out_specs=vmem(1)[0],
         scratch_shapes=[pltpu.VMEM((rows * 2, HALF, 48), jnp.bfloat16)]
-        + [pltpu.VMEM((rows * 2, 16, HALF), jnp.bfloat16)] * 3,
+        + [pltpu.VMEM((rows * 2, 16, 2 * HALF), jnp.bfloat16)] * 2,
         compiler_params=pltpu.CompilerParams(vmem_limit_bytes=48 * 2**20),
     )(near, counts, *plan, table, q_table, walls, rho)
 

time: 87.2 us -> 81.1 us (0.930)
  the two profiles are of different devices: /device:TPU:0 before, /device:TPU:25 now
where the time goes in v4:
time: 81.1 us; the launch traced here: 80.2 us
  Pallas kernels  70 us (86%)
  local copies, waits for them, and re-layouts  7.2 us (9%)
  other arithmetic  2.23 us (3%)
    pallas_call x1, Pallas kernels, forces(): pl.pallas_call(force_kernel, out_shape=jax.ShapeDtypeStruct((rho.shape[0]...  35.8 us
    pallas_call x1, Pallas kernels, shards(): remote(settle_kernel, 3, smem(2) + vmem(1), (jax.ShapeDtypeStruct((6, cel...  10.8 us
    pallas_call x1, Pallas kernels, densities(): pl.pallas_call(density_kernel, out_shape=(shape, shape) + tuple((jax.Shap...  9.98 us
    pallas_call x1, Pallas kernels, shards(): remote(fields_kernel, 1, smem(2) + vmem(4), jax.ShapeDtypeStruct((rows, 8...  7.11 us
    unnamed x20, local copies, waits for them, and re-layouts  6.7 us
    pallas_call x1, Pallas kernels, shards(): remote(pressure_kernel, 2, smem(1) + vmem(1), jax.ShapeDtypeStruct((rows,...  6.33 us

profile of v4, /device:TPU:25, one launch (start us, length us, event | category | flops | bytes accessed | tf_op | source)
XLA Modules:
  0.0 80.2 jit_solution(17448580627478089069)
XLA Ops:
  0.6 0.8 copy.15
  1.5 0.6 copy-done.5
  2.0 0.8 copy-done
  2.8 0.9 %copy-done.2 = f32[3,32,256]{2,1,0:T(8,128)S(1)} copy-done((f32[3,32,256]{2,1,0:T(8,128)S(1)}, f32[3,32,256]{2,1,0:T(8,128)}, u32[]{:S(2)}) %copy-start.2) | copy-done | bytes 98328
  3.7 0.9 %copy-done.3 = f32[3,32,256]{2,1,0:T(8,128)S(1)} copy-done((f32[3,32,256]{2,1,0:T(8,128)S(1)}, f32[3,32,256]{2,1,0:T(8,128)}, u32[]{:S(2)}) %copy-start.3) | copy-done | bytes 98328
  4.6 0.8 copy-done.4
  5.3 7.1 %shard_map.95.table = f32[56,8,256]{2,1,0:T(8,128)S(1)} custom-call(s32[32]{0:T(128)S(1)} %copy-done.5, s32[16]{0:T(128)S(1)} %reshape.123.sends, f32[3,32,256]{2,1,0:T(8,128)S(1)} %copy-done.2, f32[3,32,256]{2,1,0:T(8,128)S(1)} %copy-done.3, f32[32,256]{1,0:T(8,128)S(1)} %copy-done.4, s32[32,256]{1,0:T(8,128)S(1)} %copy-done), custom_call_target="tpu_custom_call" | custom-call | tf_op jit(solution)/shard_map/pallas_call | solution.py:511
  12.5 1.1 %compare_reduce_fusion = pred[56]{0:T(512)(128)(4,1)S(1)} fusion(f32[56,8,256]{2,1,0:T(8,128)S(1)} %shard_map.95.table), kind=kLoop, calls=%fused_computation.1 | loop fusion | flops 14280 | bytes 28728 | tf_op jit(solution)/shard_map/reduce_or | solution.py:518
  13.6 0.1 copy.14
  13.7 0.1 reshape.122.near
  13.8 10.0 %shard_map.96 = (f32[32,1,256]{2,1,0:T(1,128)S(1)}, f32[32,1,256]{2,1,0:T(1,128)S(1)}, s32[256]{0:T(256)S(1)}, s32[16]{0:T(128)S(1)}, s32[128]{0:T(128)S(1)}) custom-call(s32[96]{0:T(128)S(1)} %reshape.122.near, s32[32]{0:T(128)S(1)} %copy-done.5, s32[56]{0:T(128)S(1)} %convert_element_type.19.filled, f32[56,8,256]{2,1,0:T(8,128)S(1)} %shard_map.95.table), custom_call_target="tpu_custom_call" | custom-call | tf_op jit(solution)/shard_map/pallas_call | solution.py:437
  23.8 6.3 %shard_map.97.q_table = f32[56,1,256]{2,1,0:T(1,128)S(1)} custom-call(s32[16]{0:T(128)S(1)} %reshape.123.sends, f32[32,1,256]{2,1,0:T(1,128)S(1)} %get-tuple-element.10.pressure), custom_call_target="tpu_custom_call" | custom-call | tf_op jit(solution)/shard_map/pallas_call | solution.py:520
  30.1 35.8 %shard_map.98.moved = f32[32,8,256]{2,1,0:T(8,128)S(1)} custom-call(s32[96]{0:T(128)S(1)} %reshape.122.near, s32[32]{0:T(128)S(1)} %copy-done.5, s32[256]{0:T(256)S(1)} %get-tuple-element.7.lists, s32[16]{0:T(128)S(1)} %get-tuple-element.8.sizes, s32[128]{0:T(128)S(1)} %get-tuple-element.9.extra, f32[56,8,256]{2,1,0:T(8,128)S(1)} %shard_map.95.table, ...), custom_call_target="tpu_custom_call" | custom-call | tf_op jit(solution)/shard_map/pallas_call | solution.py:449
  65.9 0.7 copy-done.6
  66.7 0.2 convert_reduce_fusion.1
  66.9 0.2 select_reduce_fusion.1.picks
  67.2 0.1 eq.85
  67.3 0.2 convert_reduce_fusion
  67.5 0.1 convert_reduce_fusion.2
  67.6 0.1 select_reduce_fusion.2
  68.0 0.1 select_reduce_fusion.order
  68.1 10.8 %shard_map.99 = (f32[6,32,256]{2,1,0:T(8,128)S(1)}, f32[32,256]{1,0:T(8,128)S(1)}) custom-call(s32[16]{0:T(128)S(1)} %select_reduce_fusion.1.picks, s32[32]{0:T(128)S(1)} %select_reduce_fusion.order, f32[32,8,256]{2,1,0:T(8,128)S(1)} %shard_map.98.moved), custom_call_target="tpu_custom_call" | custom-call | tf_op jit(solution)/shard_map/pallas_call | solution.py:528
  78.9 0.7 copy.18
  79.6 0.6 copy.19
  (23 shorter events, 0.5 us)
Async XLA Ops:
  1.4 0.7 copy-start.5
  2.0 0.8 copy-start
  2.8 0.9 %copy-start.2 = (f32[3,32,256]{2,1,0:T(8,128)S(1)}, f32[3,32,256]{2,1,0:T(8,128)}, u32[]{:S(2)}) copy-start(f32[3,32,256]{2,1,0:T(8,128)} %pos.1) | copy-start | bytes 294916
  3.7 0.9 %copy-start.3 = (f32[3,32,256]{2,1,0:T(8,128)S(1)}, f32[3,32,256]{2,1,0:T(8,128)}, u32[]{:S(2)}) copy-start(f32[3,32,256]{2,1,0:T(8,128)} %vel.1) | copy-start | bytes 294916
  4.6 0.8 copy-start.4
  12.5 1.1 %copy-start.7 = (s32[32,3]{0,1:T(4,128)S(1)}, s32[32,3]{0,1:T(4,128)}, u32[]{:S(2)}) copy-start(s32[32,3]{0,1:T(4,128)} %param.13) | copy-start | bytes 1156
  23.8 6.3 %copy-start.1 = (s32[32,256]{1,0:T(8,128)S(1)}, s32[32,256]{1,0:T(8,128)}, u32[]{:S(2)}) copy-start(s32[32,256]{1,0:T(8,128)} %walls.3) | copy-start | bytes 98308
  65.9 0.7 copy-start.6

commit v5 on v4

--- a/solution.py
+++ b/solution.py
@@ -126,7 +126,6 @@
 
     to_peers(hello)
     if not rim:
-        pl.semaphore_wait(barrier, lax.axis_size("dev") - 1)
         return
 
     @pl.when(group > 0)
@@ -137,8 +136,13 @@
     def _():
         pl.semaphore_signal(barrier, inc=1, device_id={"group": group + 1}, device_id_type=MESH)
 
-    sides = jnp.where(group > 0, 1, 0) + jnp.where(group < groups - 1, 1, 0)
-    pl.semaphore_wait(barrier, lax.axis_size("dev") - 1 + sides)
+
+def greeted(rim):
+    group, groups = lax.axis_index("group"), lax.axis_size("group")
+    amount = lax.axis_size("dev") - 1
+    if rim:
+        amount = amount + jnp.where(group > 0, 1, 0) + jnp.where(group < groups - 1, 1, 0)
+    pl.semaphore_wait(pltpu.get_barrier_semaphore(), amount)
 
 
 def swap_slots(source, target, base, width, send_sem, recv_sem):
@@ -225,6 +229,8 @@
     base = cells + 2 * RIM_CELLS
     width = slots // lax.axis_size("dev")
 
+    greet(True)
+
     def rows(c):
         mass = masses[pl.ds(c, 1)]
         slot = lax.broadcasted_iota(jnp.int32, mass.shape, 1)
@@ -245,11 +251,11 @@
         out[s] = rows(jnp.maximum(c, 0)) * (c >= 0).astype(jnp.float32)
         return 0
 
-    lax.fori_loop(0, slots, listed, 0)
-    lax.fori_loop(0, cells, own, 0)
+    lax.fori_loop(0, slots, listed, 0, unroll=4)
+    lax.fori_loop(0, cells, own, 0, unroll=4)
     clear_missing(table, cells)
     clear_own(table, base, width)
-    greet(True)
+    greeted(True)
     done_slots = swap_slots(out, table, base, width, slot_send, slot_recv)
     done_rims = swap_rims(table, cells, rim_sem)
     done_slots()
@@ -262,6 +268,8 @@
     base = cells + 2 * RIM_CELLS
     width = slots // lax.axis_size("dev")
 
+    greet(True)
+
     def listed(s, _):
         c = sends[s]
         out[s] = pressure[jnp.maximum(c, 0)] * (c >= 0).astype(jnp.float32)
@@ -271,11 +279,11 @@
         table[RIM_CELLS + c] = pressure[c]
         return 0
 
-    lax.fori_loop(0, slots, listed, 0)
-    lax.fori_loop(0, cells, own, 0)
+    lax.fori_loop(0, slots, listed, 0, unroll=4)
+    lax.fori_loop(0, cells, own, 0, unroll=4)
     clear_missing(table, cells)
     clear_own(table, base, width)
-    greet(True)
+    greeted(True)
     done_slots = swap_slots(out, table, base, width, slot_send, slot_recv)
     done_rims = swap_rims(table, cells, rim_sem)
     done_slots()
@@ -287,6 +295,8 @@
     slots = out.shape[0]
     width = slots // lax.axis_size("dev")
 
+    greet(False)
+
     def listed(s, _):
         out[s] = moved[picks[s]]
         return 0
@@ -295,10 +305,10 @@
         pool[c] = moved[c]
         return 0
 
-    lax.fori_loop(0, slots, listed, 0)
-    lax.fori_loop(0, cells, own, 0)
+    lax.fori_loop(0, slots, listed, 0, unroll=4)
+    lax.fori_loop(0, cells, own, 0, unroll=4)
     clear_own(pool, cells, width)
-    greet(False)
+    greeted(False)
     swap_slots(out, pool, cells, width, slot_send, slot_recv)()
 
     def place(s, _):
@@ -308,7 +318,7 @@
         rho[pl.ds(s, 1)] = row[6:7]
         return 0
 
-    lax.fori_loop(0, cells, place, 0)
+    lax.fori_loop(0, cells, place, 0, unroll=4)
 
 
 def density_kernel(near, counts, filled, table, rho_ref, q_ref, lists, sizes, extra, left):

time: 81.1 us -> 79.5 us (0.980)
  the two profiles are of different devices: /device:TPU:25 before, /device:TPU:11 now
where the time goes in v5:
time: 79.5 us; the launch traced here: 80 us
  Pallas kernels  69.8 us (88%)
  local copies, waits for them, and re-layouts  7.2 us (9%)
  other arithmetic  2.23 us (3%)
    pallas_call x1, Pallas kernels, forces(): pl.pallas_call(force_kernel, out_shape=jax.ShapeDtypeStruct((rho.shape[0]...  32.2 us
    pallas_call x1, Pallas kernels, shards(): remote(settle_kernel, 3, smem(2) + vmem(1), (jax.ShapeDtypeStruct((6, cel...  15.5 us
    pallas_call x1, Pallas kernels, densities(): pl.pallas_call(density_kernel, out_shape=(shape, shape) + tuple((jax.Shap...  9.54 us
    unnamed x20, local copies, waits for them, and re-layouts  6.7 us
    pallas_call x1, Pallas kernels, shards(): remote(pressure_kernel, 2, smem(1) + vmem(1), jax.ShapeDtypeStruct((rows,...  6.32 us
    pallas_call x1, Pallas kernels, shards(): remote(fields_kernel, 1, smem(2) + vmem(4), jax.ShapeDtypeStruct((rows, 8...  6.32 us

profile of v5, /device:TPU:11, one launch (start us, length us, event | category | flops | bytes accessed | tf_op | source)
XLA Modules:
  0.0 80.0 jit_solution(12718559404974245560)
XLA Ops:
  0.6 0.8 copy.15
  1.5 0.6 copy-done.5
  2.0 0.8 copy-done
  2.8 0.9 %copy-done.2 = f32[3,32,256]{2,1,0:T(8,128)S(1)} copy-done((f32[3,32,256]{2,1,0:T(8,128)S(1)}, f32[3,32,256]{2,1,0:T(8,128)}, u32[]{:S(2)}) %copy-start.2) | copy-done | bytes 98328
  3.7 0.9 %copy-done.3 = f32[3,32,256]{2,1,0:T(8,128)S(1)} copy-done((f32[3,32,256]{2,1,0:T(8,128)S(1)}, f32[3,32,256]{2,1,0:T(8,128)}, u32[]{:S(2)}) %copy-start.3) | copy-done | bytes 98328
  4.6 0.8 copy-done.4
  5.3 6.3 %shard_map.95.table = f32[56,8,256]{2,1,0:T(8,128)S(1)} custom-call(s32[32]{0:T(128)S(1)} %copy-done.5, s32[16]{0:T(128)S(1)} %reshape.123.sends, f32[3,32,256]{2,1,0:T(8,128)S(1)} %copy-done.2, f32[3,32,256]{2,1,0:T(8,128)S(1)} %copy-done.3, f32[32,256]{1,0:T(8,128)S(1)} %copy-done.4, s32[32,256]{1,0:T(8,128)S(1)} %copy-done), custom_call_target="tpu_custom_call" | custom-call | tf_op jit(solution)/shard_map/pallas_call | solution.py:521
  11.7 1.1 %compare_reduce_fusion = pred[56]{0:T(512)(128)(4,1)S(1)} fusion(f32[56,8,256]{2,1,0:T(8,128)S(1)} %shard_map.95.table), kind=kLoop, calls=%fused_computation.1 | loop fusion | flops 14280 | bytes 28728 | tf_op jit(solution)/shard_map/reduce_or | solution.py:528
  12.8 0.1 copy.14
  12.9 0.1 reshape.122.near
  13.0 9.5 %shard_map.96 = (f32[32,1,256]{2,1,0:T(1,128)S(1)}, f32[32,1,256]{2,1,0:T(1,128)S(1)}, s32[256]{0:T(256)S(1)}, s32[16]{0:T(128)S(1)}, s32[128]{0:T(128)S(1)}) custom-call(s32[96]{0:T(128)S(1)} %reshape.122.near, s32[32]{0:T(128)S(1)} %copy-done.5, s32[56]{0:T(128)S(1)} %convert_element_type.19.filled, f32[56,8,256]{2,1,0:T(8,128)S(1)} %shard_map.95.table), custom_call_target="tpu_custom_call" | custom-call | tf_op jit(solution)/shard_map/pallas_call | solution.py:447
  22.5 6.3 %shard_map.97.q_table = f32[56,1,256]{2,1,0:T(1,128)S(1)} custom-call(s32[16]{0:T(128)S(1)} %reshape.123.sends, f32[32,1,256]{2,1,0:T(1,128)S(1)} %get-tuple-element.10.pressure), custom_call_target="tpu_custom_call" | custom-call | tf_op jit(solution)/shard_map/pallas_call | solution.py:530
  28.9 32.2 %shard_map.98.moved = f32[32,8,256]{2,1,0:T(8,128)S(1)} custom-call(s32[96]{0:T(128)S(1)} %reshape.122.near, s32[32]{0:T(128)S(1)} %copy-done.5, s32[256]{0:T(256)S(1)} %get-tuple-element.7.lists, s32[16]{0:T(128)S(1)} %get-tuple-element.8.sizes, s32[128]{0:T(128)S(1)} %get-tuple-element.9.extra, f32[56,8,256]{2,1,0:T(8,128)S(1)} %shard_map.95.table, ...), custom_call_target="tpu_custom_call" | custom-call | tf_op jit(solution)/shard_map/pallas_call | solution.py:459
  61.1 0.7 copy-done.6
  61.8 0.2 convert_reduce_fusion.1
  62.1 0.2 select_reduce_fusion.1.picks
  62.3 0.1 eq.85
  62.4 0.2 convert_reduce_fusion
  62.6 0.1 convert_reduce_fusion.2
  62.7 0.1 select_reduce_fusion.2
  63.1 0.1 select_reduce_fusion.order
  63.2 15.5 %shard_map.99 = (f32[6,32,256]{2,1,0:T(8,128)S(1)}, f32[32,256]{1,0:T(8,128)S(1)}) custom-call(s32[16]{0:T(128)S(1)} %select_reduce_fusion.1.picks, s32[32]{0:T(128)S(1)} %select_reduce_fusion.order, f32[32,8,256]{2,1,0:T(8,128)S(1)} %shard_map.98.moved), custom_call_target="tpu_custom_call" | custom-call | tf_op jit(solution)/shard_map/pallas_call | solution.py:538
  78.7 0.7 copy.18
  79.4 0.6 copy.19
  (23 shorter events, 0.5 us)
Async XLA Ops:
  1.4 0.7 copy-start.5
  2.0 0.8 copy-start
  2.8 0.9 %copy-start.2 = (f32[3,32,256]{2,1,0:T(8,128)S(1)}, f32[3,32,256]{2,1,0:T(8,128)}, u32[]{:S(2)}) copy-start(f32[3,32,256]{2,1,0:T(8,128)} %pos.1) | copy-start | bytes 294916
  3.7 0.9 %copy-start.3 = (f32[3,32,256]{2,1,0:T(8,128)S(1)}, f32[3,32,256]{2,1,0:T(8,128)}, u32[]{:S(2)}) copy-start(f32[3,32,256]{2,1,0:T(8,128)} %vel.1) | copy-start | bytes 294916
  4.6 0.8 copy-start.4
  11.7 1.1 %copy-start.7 = (s32[32,3]{0,1:T(4,128)S(1)}, s32[32,3]{0,1:T(4,128)}, u32[]{:S(2)}) copy-start(s32[32,3]{0,1:T(4,128)} %param.13) | copy-start | bytes 1156
  22.5 6.3 %copy-start.1 = (s32[32,256]{1,0:T(8,128)S(1)}, s32[32,256]{1,0:T(8,128)}, u32[]{:S(2)}) copy-start(s32[32,256]{1,0:T(8,128)} %walls.3) | copy-start | bytes 98308
  61.1 0.7 copy-start.6

commit v6 on v5

--- a/solution.py
+++ b/solution.py
@@ -429,7 +429,7 @@
             active * jnp.concatenate([new_pos, new_vel, rho, jnp.zeros_like(rho)], 0), full
         )
 
-    by_class(lists, sizes, cell, 1)
+    by_class(lists, sizes, cell, 2)
 
 
 def vmem(count):

time: 79.5 us -> 83.3 us (1.048)
  the two profiles are of different devices: /device:TPU:11 before, /device:TPU:0 now
where the time goes in v6:
time: 83.3 us; the launch traced here: 84.8 us
  Pallas kernels  74.7 us (90%)
  local copies, waits for them, and re-layouts  7.2 us (9%)
  other arithmetic  2.23 us (3%)
    pallas_call x1, Pallas kernels, forces(): pl.pallas_call(force_kernel, out_shape=jax.ShapeDtypeStruct((rho.shape[0]...  32.8 us
    pallas_call x1, Pallas kernels, shards(): remote(settle_kernel, 3, smem(2) + vmem(1), (jax.ShapeDtypeStruct((6, cel...  17.5 us
    pallas_call x1, Pallas kernels, densities(): pl.pallas_call(density_kernel, out_shape=(shape, shape) + tuple((jax.Shap...  10.1 us
    pallas_call x1, Pallas kernels, shards(): remote(fields_kernel, 1, smem(2) + vmem(4), jax.ShapeDtypeStruct((rows, 8...  8.14 us
    unnamed x20, local copies, waits for them, and re-layouts  6.7 us
    pallas_call x1, Pallas kernels, shards(): remote(pressure_kernel, 2, smem(1) + vmem(1), jax.ShapeDtypeStruct((rows,...  6.05 us

profile of v6, /device:TPU:0, one launch (start us, length us, event | category | flops | bytes accessed | tf_op | source)
XLA Modules:
  0.0 84.8 jit_solution(5552093660102440681)
XLA Ops:
  0.6 0.8 copy.15
  1.5 0.6 copy-done.5
  2.0 0.8 copy-done
  2.8 0.9 %copy-done.2 = f32[3,32,256]{2,1,0:T(8,128)S(1)} copy-done((f32[3,32,256]{2,1,0:T(8,128)S(1)}, f32[3,32,256]{2,1,0:T(8,128)}, u32[]{:S(2)}) %copy-start.2) | copy-done | bytes 98328
  3.7 0.9 %copy-done.3 = f32[3,32,256]{2,1,0:T(8,128)S(1)} copy-done((f32[3,32,256]{2,1,0:T(8,128)S(1)}, f32[3,32,256]{2,1,0:T(8,128)}, u32[]{:S(2)}) %copy-start.3) | copy-done | bytes 98328
  4.6 0.8 copy-done.4
  5.3 8.1 %shard_map.95.table = f32[56,8,256]{2,1,0:T(8,128)S(1)} custom-call(s32[32]{0:T(128)S(1)} %copy-done.5, s32[16]{0:T(128)S(1)} %reshape.123.sends, f32[3,32,256]{2,1,0:T(8,128)S(1)} %copy-done.2, f32[3,32,256]{2,1,0:T(8,128)S(1)} %copy-done.3, f32[32,256]{1,0:T(8,128)S(1)} %copy-done.4, s32[32,256]{1,0:T(8,128)S(1)} %copy-done), custom_call_target="tpu_custom_call" | custom-call | tf_op jit(solution)/shard_map/pallas_call | solution.py:521
  13.5 1.1 %compare_reduce_fusion = pred[56]{0:T(512)(128)(4,1)S(1)} fusion(f32[56,8,256]{2,1,0:T(8,128)S(1)} %shard_map.95.table), kind=kLoop, calls=%fused_computation.1 | loop fusion | flops 14280 | bytes 28728 | tf_op jit(solution)/shard_map/reduce_or | solution.py:528
  14.6 0.1 copy.14
  14.7 0.1 reshape.122.near
  14.8 10.1 %shard_map.96 = (f32[32,1,256]{2,1,0:T(1,128)S(1)}, f32[32,1,256]{2,1,0:T(1,128)S(1)}, s32[256]{0:T(256)S(1)}, s32[16]{0:T(128)S(1)}, s32[128]{0:T(128)S(1)}) custom-call(s32[96]{0:T(128)S(1)} %reshape.122.near, s32[32]{0:T(128)S(1)} %copy-done.5, s32[56]{0:T(128)S(1)} %convert_element_type.19.filled, f32[56,8,256]{2,1,0:T(8,128)S(1)} %shard_map.95.table), custom_call_target="tpu_custom_call" | custom-call | tf_op jit(solution)/shard_map/pallas_call | solution.py:447
  25.0 6.0 %shard_map.97.q_table = f32[56,1,256]{2,1,0:T(1,128)S(1)} custom-call(s32[16]{0:T(128)S(1)} %reshape.123.sends, f32[32,1,256]{2,1,0:T(1,128)S(1)} %get-tuple-element.10.pressure), custom_call_target="tpu_custom_call" | custom-call | tf_op jit(solution)/shard_map/pallas_call | solution.py:530
  31.0 32.8 %shard_map.98.moved = f32[32,8,256]{2,1,0:T(8,128)S(1)} custom-call(s32[96]{0:T(128)S(1)} %reshape.122.near, s32[32]{0:T(128)S(1)} %copy-done.5, s32[256]{0:T(256)S(1)} %get-tuple-element.7.lists, s32[16]{0:T(128)S(1)} %get-tuple-element.8.sizes, s32[128]{0:T(128)S(1)} %get-tuple-element.9.extra, f32[56,8,256]{2,1,0:T(8,128)S(1)} %shard_map.95.table, ...), custom_call_target="tpu_custom_call" | custom-call | tf_op jit(solution)/shard_map/pallas_call | solution.py:459
  63.8 0.7 copy-done.6
  64.6 0.2 convert_reduce_fusion.1
  64.8 0.2 select_reduce_fusion.1.picks
  65.1 0.1 eq.85
  65.2 0.2 convert_reduce_fusion
  65.4 0.1 convert_reduce_fusion.2
  65.5 0.1 select_reduce_fusion.2
  65.9 0.1 select_reduce_fusion.order
  66.0 17.5 %shard_map.99 = (f32[6,32,256]{2,1,0:T(8,128)S(1)}, f32[32,256]{1,0:T(8,128)S(1)}) custom-call(s32[16]{0:T(128)S(1)} %select_reduce_fusion.1.picks, s32[32]{0:T(128)S(1)} %select_reduce_fusion.order, f32[32,8,256]{2,1,0:T(8,128)S(1)} %shard_map.98.moved), custom_call_target="tpu_custom_call" | custom-call | tf_op jit(solution)/shard_map/pallas_call | solution.py:538
  83.5 0.7 copy.18
  84.2 0.6 copy.19
  (23 shorter events, 0.5 us)
Async XLA Ops:
  1.4 0.7 copy-start.5
  2.0 0.8 copy-start
  2.8 0.9 %copy-start.2 = (f32[3,32,256]{2,1,0:T(8,128)S(1)}, f32[3,32,256]{2,1,0:T(8,128)}, u32[]{:S(2)}) copy-start(f32[3,32,256]{2,1,0:T(8,128)} %pos.1) | copy-start | bytes 294916
  3.7 0.9 %copy-start.3 = (f32[3,32,256]{2,1,0:T(8,128)S(1)}, f32[3,32,256]{2,1,0:T(8,128)}, u32[]{:S(2)}) copy-start(f32[3,32,256]{2,1,0:T(8,128)} %vel.1) | copy-start | bytes 294916
  4.6 0.8 copy-start.4
  13.5 1.1 %copy-start.7 = (s32[32,3]{0,1:T(4,128)S(1)}, s32[32,3]{0,1:T(4,128)}, u32[]{:S(2)}) copy-start(s32[32,3]{0,1:T(4,128)} %param.13) | copy-start | bytes 1156
  25.0 6.1 %copy-start.1 = (s32[32,256]{1,0:T(8,128)S(1)}, s32[32,256]{1,0:T(8,128)}, u32[]{:S(2)}) copy-start(s32[32,256]{1,0:T(8,128)} %walls.3) | copy-start | bytes 98308
  63.8 0.7 copy-start.6
